TPU v7x, 512 devices: a whole 4x8x8 slice. The times are simulated.
512 devices in a mesh: grp: 16 (over y_lo, z), sub: 32 (over y_hi, x, core).
Axes of the slice: x: 4, y: 8 (y_hi: 4, y_lo: 2; y = y_hi * 2 + y_lo), z: 8, core: 2. Of those that a mesh axis runs over, the one named last changes fastest.
Arguments:
- phase_labels: int32 [512, 1152], P(('grp', 'sub')), may hold values from 0 to 2
- phase_perm: float32 [3], replicated, may hold values from 0.2 to 5
- local_inverse: bfloat16 [512, 1152, 1152], P(('grp', 'sub')), may hold values from -0.1875 to 0.1875
- sources: bfloat16 [512, 256, 1152], P(('grp', 'sub')), may hold values from -6 to 6
- shift: float32 [512, 256], P(('grp', 'sub')), may hold values from 1 to 30
- probe: float32 [256, 8], replicated, may hold values from -48 to 48
Outputs:
- coefficients: float32 [512, 256, 8], P(('grp', 'sub'))
- element_stiffness: float32 [512, 32, 32], P(('grp', 'sub'))
All inputs are finite; a program needn't handle non-finite values.
Results may differ from a plain program's by a relative error of at most 0.0055.
Values may be sent and summed in bfloat16 or wider, within the bound.
A program may use at most 64 MiB of HBM per device.

v0:
```python
import jax
import jax.numpy as jnp
from jax import lax
from jax.sharding import PartitionSpec as P

CELLX = 12
CELLY = 12
CELLZ = 8
SNAP = 256
NBASIS = 8
PHASES = 3
NCELL = 1152


HIGH_PRECISION = lax.Precision.HIGHEST


def passed_along(block, axis, distance):
    devices = range(lax.axis_size(axis))
    route = [((i - distance) % len(devices), i) for i in devices]
    return lax.ppermute(block, axis, route)


def weights_of(material_labels, phase_perm):
    cell_index = jnp.arange(NCELL, dtype=jnp.int32)
    coord_x = cell_index // (CELLY * CELLZ)
    coord_y = cell_index // CELLZ % CELLY
    coord_z = cell_index % CELLZ
    frac_x = (coord_x.astype(jnp.float32) + 0.5) / CELLX
    frac_y = (coord_y.astype(jnp.float32) + 0.5) / CELLY
    partition = jnp.stack(
        [
            (1.0 - frac_x) * (1.0 - frac_y),
            frac_x * (1.0 - frac_y),
            (1.0 - frac_x) * frac_y,
            frac_x * frac_y,
        ]
    )
    onehot = (material_labels[None, :] == jnp.arange(PHASES, dtype=jnp.int32)[:, None]).astype(
        jnp.float32
    )
    cell_permeability = jnp.sum(onehot * phase_perm[:, None], axis=0)
    face_list = []
    weight_list = []
    for stride, coordinate, limit in (
        (CELLY * CELLZ, coord_x, CELLX),
        (CELLZ, coord_y, CELLY),
        (1, coord_z, CELLZ),
    ):
        neighbour_permeability = jnp.roll(cell_permeability, -stride)
        inside = (coordinate < limit - 1).astype(jnp.float32)
        face_kappa = (
            2.0
            * cell_permeability
            * neighbour_permeability
            / (cell_permeability + neighbour_permeability)
            * inside
        )
        face_list.append(face_kappa)
        weight_list.append(
            face_kappa[None, :] * 0.5 * (partition + jnp.roll(partition, -stride, axis=1))
        )
    return (
        partition,
        jnp.stack(face_list),
        cell_permeability[None, :] * partition,
        jnp.stack(weight_list),
    )


def differences(field):
    return jnp.stack(
        [jnp.roll(field, -stride, axis=-1) - field for stride in (CELLY * CELLZ, CELLZ, 1)]
    )


def local(phase_labels, phase_perm, local_inverse, sources, shift, probe):
    volume = 1.0 / NCELL
    partition, face_kappa, mass_weight, face_weight = weights_of(phase_labels[0], phase_perm)
    snapshot_fields = jnp.dot(
        sources[0], local_inverse[0], preferred_element_type=jnp.float32
    ).astype(jnp.bfloat16)
    gradients = differences(snapshot_fields.astype(jnp.float32)).astype(jnp.bfloat16)
    mass_weighted = (snapshot_fields[None] * (mass_weight * volume)[:, None, :]).astype(
        jnp.bfloat16
    )
    mass_gram = jnp.einsum(
        "csn,tn->cst", mass_weighted, snapshot_fields, preferred_element_type=jnp.float32
    )
    grad_weighted = (gradients[:, None] * (face_weight * volume)[:, :, None, :]).astype(
        jnp.bfloat16
    )
    stiffness = jnp.einsum(
        "dcsn,dtn->cst", grad_weighted, gradients, preferred_element_type=jnp.float32
    )
    came_stiff, came_mass = passed_along((stiffness[1::2], mass_gram[1::2]), "sub", 1)
    row_stiff = stiffness[0::2] + came_stiff
    row_mass = mass_gram[0::2] + came_mass
    below_stiff, below_mass = passed_along((row_stiff[1], row_mass[1]), "grp", 1)
    node_stiff = row_stiff[0] + below_stiff
    node_mass = row_mass[0] + below_mass
    right_side = jnp.dot(node_mass, probe, precision=HIGH_PRECISION)
    cholesky_factor = jnp.linalg.cholesky(node_stiff + jnp.diag(shift[0]))
    coefficients = jax.scipy.linalg.cho_solve((cholesky_factor, True), right_side)
    own_coef = coefficients.astype(jnp.bfloat16)
    upper_coef = passed_along(own_coef, "grp", -1)
    right_coef, diagonal_coef = passed_along((own_coef, upper_coef), "sub", -1)
    corner_coefficient = jnp.stack([own_coef, right_coef, upper_coef, diagonal_coef])
    field_projection = jnp.einsum(
        "wrp,rd->wpd", corner_coefficient, snapshot_fields, preferred_element_type=jnp.float32
    )
    basis_field = (field_projection * partition[:, None, :]).reshape(4 * NBASIS, NCELL)
    slopes = differences(basis_field)
    element_stiffness = jnp.einsum(
        "dan,dbn->ab", slopes * face_kappa[:, None, :], slopes, precision=HIGH_PRECISION
    ) / (NCELL * SNAP)
    return (coefficients[None], element_stiffness[None])


def solution(mesh):
    in_specs = (
        P(("grp", "sub"), None),
        P(),
        P(("grp", "sub"), None, None),
        P(("grp", "sub"), None, None),
        P(("grp", "sub"), None),
        P(),
    )
    out_specs = (P(("grp", "sub"), None, None), P(("grp", "sub"), None, None))
    return jax.shard_map(local, mesh=mesh, in_specs=in_specs, out_specs=out_specs, check_vma=False)
```

profile of v0, /device:TPU:31, one launch (start us, length us, event | category | flops | bytes accessed | tf_op | source)
XLA Modules:
  0.0 151.7 jit_solution(9545332078942180036)
XLA Ops:
  2.4 2.1 %fusion.89 = (f32[256,1152]{1,0:T(8,128)S(1)}, bf16[256,1152]{1,0:T(8,128)(2,1)S(1)}) fusion(bf16[1,1152,1152]{2,1,0:T(8,128)(2,1)S(1)} %copy-done, bf16[1,256,1152]{2,1,0:T(8,128)(2,1)} %param.9), kind=kOutput, calls=%fused_computation.185 | convolution fusion | flops 680067072 | bytes 5013504 | tf_op jit(solution)/shard_map/dot_general | solution.py:80
  6.3 5.0 %collective-permute-start.2 = (f32[2,256,256]{2,1,0:T(8,128)}, f32[2,256,256]{2,1,0:T(8,128)}, u32[]{:S(2)}, u32[]{:S(2)}) collective-permute-start(f32[2,256,256]{2,1,0:T(8,128)} %slice.205), channel_id=1, source_target_pairs={{31,0},{0,1},{1,2},{2,3},{3,4},{4,5},{5,6},{6,7},{7,8},{8,9},{9,10... | collective-permute-start | bytes 1572872 | tf_op jit(solution)/shard_map/ppermute | solution.py:21
  14.9 2.1 %fusion.12 = f32[4,256,256]{1,2,0:T(8,128)S(1)} fusion(f32[3,4,1152]{2,0,1:T(4,128)S(1)} %copy.45, f32[3,256,1152]{2,1,0:T(8,128)S(1)} %fusion.20, bf16[1,256,1152]{2,1,0:T(8,128)(2,1)S(1)} %get-tuple-element.38, bf16[1,256,1152]{2,1,0:T(8,128)(2,1)S(1)} %get-tuple-element.37, bf16[1,256,1152]{2,1,0:T(8,128)(2,1)S(1)} %get-tuple-element.36), kind=kOutput, calls=%fused_computation.16 | convolution fusion | flops 1820786688 | bytes 6412288 | tf_op jit(solution)/shard_map/dcsn,dtn->cst/dot_general | solution.py:93
  17.0 1.0 copy-done.1
  18.9 1.9 %collective-permute-start = (f32[2,256,256]{1,2,0:T(8,128)}, f32[2,256,256]{1,2,0:T(8,128)}, u32[]{:S(2)}, u32[]{:S(2)}) collective-permute-start(f32[2,256,256]{1,2,0:T(8,128)} %slice.201), channel_id=1, source_target_pairs={{31,0},{0,1},{1,2},{2,3},{3,4},{4,5},{5,6},{6,7},{7,8},{8,9},{9,10... | collective-permute-start | bytes 1572872 | tf_op jit(solution)/shard_map/ppermute | solution.py:21
  22.2 11.9 %collective-permute-done = f32[2,256,256]{1,2,0:T(8,128)} collective-permute-done((f32[2,256,256]{1,2,0:T(8,128)}, f32[2,256,256]{1,2,0:T(8,128)}, u32[]{:S(2)}, u32[]{:S(2)}) %collective-permute-start) | collective-permute-done | bytes 524320 | tf_op jit(solution)/shard_map/ppermute | solution.py:21
  34.1 1.3 slice_add_fusion.1
  35.4 1.9 %collective-permute-start.1 = (f32[256,256]{0,1:T(8,128)S(1)}, f32[256,256]{0,1:T(8,128)S(1)}, u32[]{:S(2)}, u32[]{:S(2)}) collective-permute-start(f32[256,256]{0,1:T(8,128)S(1)} %slice_bitcast_fusion.2), channel_id=1, source_target_pairs={{480,0},{0,32},{32,64},{64,96},{96,128},{128,160},{160,192},{192,2... | collective-permute-start | bytes 786440 | tf_op jit(solution)/shard_map/ppermute | solution.py:21
  37.3 1.1 slice_add_fusion
  39.2 2.1 %collective-permute-start.3 = (f32[256,256]{1,0:T(8,128)}, f32[256,256]{1,0:T(8,128)}, u32[]{:S(2)}, u32[]{:S(2)}) collective-permute-start(f32[256,256]{1,0:T(8,128)} %slice_bitcast_fusion), channel_id=1, source_target_pairs={{480,0},{0,32},{32,64},{64,96},{96,128},{128,160},{160,192},{192,2... | collective-permute-start | bytes 786440 | tf_op jit(solution)/shard_map/ppermute | solution.py:21
  41.3 13.8 %collective-permute-done.1 = f32[256,256]{0,1:T(8,128)S(1)} collective-permute-done((f32[256,256]{0,1:T(8,128)S(1)}, f32[256,256]{0,1:T(8,128)S(1)}, u32[]{:S(2)}, u32[]{:S(2)}) %collective-permute-start.1) | collective-permute-done | bytes 262176 | tf_op jit(solution)/shard_map/ppermute | solution.py:21
  56.1 1.0 fusion.38
  57.8 11.7 %cholesky.49 = f32[128,128]{1,0:T(8,128)S(1)} custom-call(f32[128,128]{1,0:T(8,128)S(1)} %cholesky.115), custom_call_target="Cholesky" | custom-call | tf_op jit(solution)/shard_map/jit(cholesky)/cholesky | solution.py:103
  70.1 9.8 %custom-call.18 = f32[1,128,128]{1,2,0:T(8,128)S(1)} custom-call(f32[1,128,128]{2,1,0:T(8,128)S(1)} %get-tuple-element.43), custom_call_target="InvertDiagBlocksLowerTriangular" | custom-call | tf_op jit(solution)/shard_map/jit(cholesky)/cholesky | solution.py:103
  80.0 1.0 fusion.40
  81.0 1.7 %convolution_subtract_fusion = f32[128,128]{1,0:T(8,128)} fusion(f32[128,128]{1,0:T(8,128)S(1)} %fusion.40, f32[256,256]{1,0:T(8,128)} %copy-done.5), kind=kOutput, calls=%fused_computation.23 | convolution fusion | flops 25182208 | bytes 262144 | tf_op jit(solution)/shard_map/jit(cholesky)/cholesky | solution.py:103
  82.8 12.6 %cholesky.103 = f32[128,128]{1,0:T(8,128)S(1)} custom-call(f32[128,128]{1,0:T(8,128)} %convolution_subtract_fusion), custom_call_target="Cholesky" | custom-call | tf_op jit(solution)/shard_map/jit(cholesky)/cholesky | solution.py:103
  96.1 1.3 compare_reduce_fusion.1
  97.4 1.3 compare_reduce_fusion
  101.5 7.0 %while.1 = (s32[]{:T(128)}, f32[256,256]{0,1:T(8,128)}, s32[2,2]{1,0:T(2,128)S(1)}, f32[2,128,128]{2,1,0:T(8,128)}, s32[]{:T(128)}) while((s32[]{:T(128)}, f32[256,256]{0,1:T(8,128)}, s32[2,2]{1,0:T(2,128)S(1)}, f32[2,128,128]{2,1,0:T(8,128)}, s32[]{:T(128)}) %tuple.45), condition=%wide.while_cond, body=%wide.while_body.sunk | while | flops 2 | bytes 393329 | solution.py:104
  102.1 2.2 %dynamic-slice.7 = f32[128,128]{0,1:T(8,128)S(1)} dynamic-slice(f32[256,256]{0,1:T(8,128)} %get-tuple-element.108, s32[]{:T(128)} %bitcast.139, s32[]{:T(128)} %bitcast.140), dynamic_slice_sizes={128,128} | dynamic-slice | bytes 131076 | tf_op jit(solution)/shard_map/jit(_cho_solve)/triangular_solve
  105.6 2.1 %dynamic-slice.7 = f32[128,128]{0,1:T(8,128)S(1)} dynamic-slice(f32[256,256]{0,1:T(8,128)} %get-tuple-element.108, s32[]{:T(128)} %bitcast.139, s32[]{:T(128)} %bitcast.140), dynamic_slice_sizes={128,128} | dynamic-slice | bytes 131076 | tf_op jit(solution)/shard_map/jit(_cho_solve)/triangular_solve
  108.5 20.5 %custom-call.19 = f32[2,128,128]{1,2,0:T(8,128)S(1)} custom-call(f32[2,128,128]{2,1,0:T(8,128)} %get-tuple-element.9), custom_call_target="InvertDiagBlocksLowerTriangular" | custom-call | tf_op jit(solution)/shard_map/jit(_cho_solve)/triangular_solve | solution.py:104
  129.0 1.3 fusion.34
  130.5 1.0 fusion.48
  131.9 1.1 convolution_subtract_fusion.1
  133.2 3.4 %collective-permute-start.5 = (bf16[256,8]{0,1:T(8,128)(2,1)S(1)}, bf16[256,8]{0,1:T(8,128)(2,1)S(1)}, u32[]{:S(2)}, u32[]{:S(2)}) collective-permute-start(bf16[256,8]{0,1:T(8,128)(2,1)S(1)} %fusion.76), channel_id=1, source_target_pairs={{32,0},{64,32},{96,64},{128,96},{160,128},{192,160},{224,192},{256... | collective-permute-start | bytes 12296 | tf_op jit(solution)/shard_map/ppermute | solution.py:21
  136.6 1.9 %collective-permute-start.4 = (bf16[256,8]{0,1:T(8,128)(2,1)S(1)}, bf16[256,8]{0,1:T(8,128)(2,1)S(1)}, u32[]{:S(2)}, u32[]{:S(2)}) collective-permute-start(bf16[256,8]{0,1:T(8,128)(2,1)S(1)} %fusion.76), channel_id=1, source_target_pairs={{1,0},{2,1},{3,2},{4,3},{5,4},{6,5},{7,6},{8,7},{9,8},{10,9},{11,1... | collective-permute-start | bytes 12296 | tf_op jit(solution)/shard_map/ppermute | solution.py:21
  138.5 1.9 %collective-permute-start.6 = (bf16[256,8]{0,1:T(8,128)(2,1)S(1)}, bf16[256,8]{0,1:T(8,128)(2,1)S(1)}, u32[]{:S(2)}, u32[]{:S(2)}) collective-permute-start(bf16[256,8]{0,1:T(8,128)(2,1)S(1)} %collective-permute-done.5), channel_id=1, source_target_pairs={{1,0},{2,1},{3,2},{4,3},{5,4},{6,5},{7,6},{8,7},{9,8},{10,9},{11,1... | collective-permute-start | bytes 12296 | tf_op jit(solution)/shard_map/ppermute | solution.py:21
  141.1 6.9 %collective-permute-done.4 = bf16[256,8]{0,1:T(8,128)(2,1)S(1)} collective-permute-done((bf16[256,8]{0,1:T(8,128)(2,1)S(1)}, bf16[256,8]{0,1:T(8,128)(2,1)S(1)}, u32[]{:S(2)}, u32[]{:S(2)}) %collective-permute-start.4) | collective-permute-done | bytes 4128 | tf_op jit(solution)/shard_map/ppermute | solution.py:21
  147.9 1.9 %collective-permute-done.6 = bf16[256,8]{0,1:T(8,128)(2,1)S(1)} collective-permute-done((bf16[256,8]{0,1:T(8,128)(2,1)S(1)}, bf16[256,8]{0,1:T(8,128)(2,1)S(1)}, u32[]{:S(2)}, u32[]{:S(2)}) %collective-permute-start.6) | collective-permute-done | bytes 4128 | tf_op jit(solution)/shard_map/ppermute | solution.py:21
  150.5 1.2 fusion.19
  (99 shorter events, 19.2 us)
Async XLA Ops:
  0.6 1.8 %copy-start = (bf16[1,1152,1152]{2,1,0:T(8,128)(2,1)S(1)}, bf16[1,1152,1152]{2,1,0:T(8,128)(2,1)}, u32[]{:S(2)}) copy-start(bf16[1,1152,1152]{2,1,0:T(8,128)(2,1)} %param.8) | copy-start | bytes 7962628
  5.4 7.3 %copy-start.3 = (f32[4,256,256]{2,1,0:T(8,128)}, f32[4,256,256]{2,1,0:T(8,128)S(1)}, u32[]{:S(2)}) copy-start(f32[4,256,256]{2,1,0:T(8,128)S(1)} %fusion.8) | copy-start | bytes 3145732
  6.3 31.0 %collective-permute-start.2 = (f32[2,256,256]{2,1,0:T(8,128)}, f32[2,256,256]{2,1,0:T(8,128)}, u32[]{:S(2)}, u32[]{:S(2)}) collective-permute-start(f32[2,256,256]{2,1,0:T(8,128)} %slice.205), channel_id=1, source_target_pairs={{31,0},{0,1},{1,2},{2,3},{3,4},{4,5},{5,6},{6,7},{7,8},{8,9},{9,10... | collective-permute-start | bytes 1572872 | tf_op jit(solution)/shard_map/ppermute | solution.py:21
  17.0 1.0 copy-start.1
  18.9 15.2 %collective-permute-start = (f32[2,256,256]{1,2,0:T(8,128)}, f32[2,256,256]{1,2,0:T(8,128)}, u32[]{:S(2)}, u32[]{:S(2)}) collective-permute-start(f32[2,256,256]{1,2,0:T(8,128)} %slice.201), channel_id=1, source_target_pairs={{31,0},{0,1},{1,2},{2,3},{3,4},{4,5},{5,6},{6,7},{7,8},{8,9},{9,10... | collective-permute-start | bytes 1572872 | tf_op jit(solution)/shard_map/ppermute | solution.py:21
  22.1 15.2 %copy-start.4 = (f32[4,256,256]{2,1,0:T(8,128)S(1)}, f32[4,256,256]{2,1,0:T(8,128)}, u32[]{:S(2)}) copy-start(f32[4,256,256]{2,1,0:T(8,128)} %copy-done.3) | copy-start | bytes 3145732
  22.2 33.0 %copy-start.7 = (f32[1,256]{1,0:T(1,128)S(1)}, f32[1,256]{1,0:T(1,128)}, u32[]{:S(2)}) copy-start(f32[1,256]{1,0:T(1,128)} %param.10) | copy-start | bytes 3076
  35.4 19.8 %collective-permute-start.1 = (f32[256,256]{0,1:T(8,128)S(1)}, f32[256,256]{0,1:T(8,128)S(1)}, u32[]{:S(2)}, u32[]{:S(2)}) collective-permute-start(f32[256,256]{0,1:T(8,128)S(1)} %slice_bitcast_fusion.2), channel_id=1, source_target_pairs={{480,0},{0,32},{32,64},{64,96},{96,128},{128,160},{160,192},{192,2... | collective-permute-start | bytes 786440 | tf_op jit(solution)/shard_map/ppermute | solution.py:21
  38.5 16.7 %copy-start.2 = (f32[2,256,256]{2,1,0:T(8,128)}, f32[2,256,256]{2,1,0:T(8,128)S(1)}, u32[]{:S(2)}) copy-start(f32[2,256,256]{2,1,0:T(8,128)S(1)} %slice_add_fusion) | copy-start | bytes 1572868
  39.2 89.8 %collective-permute-start.3 = (f32[256,256]{1,0:T(8,128)}, f32[256,256]{1,0:T(8,128)}, u32[]{:S(2)}, u32[]{:S(2)}) collective-permute-start(f32[256,256]{1,0:T(8,128)} %slice_bitcast_fusion), channel_id=1, source_target_pairs={{480,0},{0,32},{32,64},{64,96},{96,128},{128,160},{160,192},{192,2... | collective-permute-start | bytes 786440 | tf_op jit(solution)/shard_map/ppermute | solution.py:21
  57.1 0.7 copy-start.5
  82.8 46.2 %copy-start.6 = (f32[256,8]{0,1:T(8,128)S(1)}, f32[256,8]{0,1:T(8,128)}, u32[]{:S(2)}) copy-start(f32[256,8]{0,1:T(8,128)} %param.11) | copy-start | bytes 24580
  133.2 5.3 %collective-permute-start.5 = (bf16[256,8]{0,1:T(8,128)(2,1)S(1)}, bf16[256,8]{0,1:T(8,128)(2,1)S(1)}, u32[]{:S(2)}, u32[]{:S(2)}) collective-permute-start(bf16[256,8]{0,1:T(8,128)(2,1)S(1)} %fusion.76), channel_id=1, source_target_pairs={{32,0},{64,32},{96,64},{128,96},{160,128},{192,160},{224,192},{256... | collective-permute-start | bytes 12296 | tf_op jit(solution)/shard_map/ppermute | solution.py:21
  136.6 11.3 %collective-permute-start.4 = (bf16[256,8]{0,1:T(8,128)(2,1)S(1)}, bf16[256,8]{0,1:T(8,128)(2,1)S(1)}, u32[]{:S(2)}, u32[]{:S(2)}) collective-permute-start(bf16[256,8]{0,1:T(8,128)(2,1)S(1)} %fusion.76), channel_id=1, source_target_pairs={{1,0},{2,1},{3,2},{4,3},{5,4},{6,5},{7,6},{8,7},{9,8},{10,9},{11,1... | collective-permute-start | bytes 12296 | tf_op jit(solution)/shard_map/ppermute | solution.py:21
  138.5 11.3 %collective-permute-start.6 = (bf16[256,8]{0,1:T(8,128)(2,1)S(1)}, bf16[256,8]{0,1:T(8,128)(2,1)S(1)}, u32[]{:S(2)}, u32[]{:S(2)}) collective-permute-start(bf16[256,8]{0,1:T(8,128)(2,1)S(1)} %collective-permute-done.5), channel_id=1, source_target_pairs={{1,0},{2,1},{3,2},{4,3},{5,4},{6,5},{7,6},{8,7},{9,8},{10,9},{11,1... | collective-permute-start | bytes 12296 | tf_op jit(solution)/shard_map/ppermute | solution.py:21
where the time goes:
time: 153 us; the launch traced here: 152 us
  other arithmetic  68 us (44%)
  waiting for transfers between devices  34.6 us (23%)
  starting transfers between devices  18.1 us (12%)
  local copies, waits for them, and re-layouts  15.2 us (10%)
  matrix products  13.4 us (9%)
  between operations  2.37 us (2%)
    another operation x7, other arithmetic, local(): cholesky_factor = jnp.linalg.cholesky(node_stiff + jnp.diag(shift[0]))  37.9 us
    ppermute x7, waiting for transfers between devices, passed_along(): return lax.ppermute(block, axis, route)  34.6 us
    another operation x5, other arithmetic, local(): jax.scipy.linalg.cho_solve((cholesky_factor, True), right_side)  21.8 us
    ppermute x7, starting transfers between devices, passed_along(): return lax.ppermute(block, axis, route)  18.1 us
    another operation x10, local copies, waits for them, and re-layouts  6.96 us
  transfers between devices with their start and end apart: 7, of which 4 were waited for; matrix products, arithmetic and copies ran while one was open for 55% of the time, Pallas kernels for 0%

commit v1 on v0

--- a/solution.py
+++ b/solution.py
@@ -1,6 +1,8 @@
 import jax
 import jax.numpy as jnp
 from jax import lax
+from jax.experimental import pallas as pl
+from jax.experimental.pallas import tpu as pltpu
 from jax.sharding import PartitionSpec as P
 
 CELLX = 12
@@ -13,6 +15,82 @@
 
 
 HIGH_PRECISION = lax.Precision.HIGHEST
+HI = HIGH_PRECISION
+N = SNAP
+NB = 16
+W = 384
+
+
+def leaf(cols, slabs, nb):
+    rows = lax.broadcasted_iota(jnp.int32, (nb, 128), 0)
+    cols = list(cols)
+    slabs = list(slabs)
+    for p in range(0, nb, 2):
+        c0, c1 = cols[p], cols[p + 1]
+        a, b = c0[p:p + 1], c1[p:p + 1]
+        bt, d = c0[p + 1:p + 2], c1[p + 1:p + 2]
+        inv = 1.0 / (a * d - b * bt)
+        a, b, bt, d = a * inv, b * inv, bt * inv, d * inv
+        top, bottom = rows == p, rows == p + 1
+        def step(t):
+            r0, r1 = t[p:p + 1], t[p + 1:p + 2]
+            s0 = d * r0 - b * r1
+            s1 = a * r1 - bt * r0
+            return jnp.where(top, s0, jnp.where(bottom, s1, t - c0 * s0 - c1 * s1))
+        for q in range(p + 2, nb):
+            cols[q] = step(cols[q])
+        slabs = [step(t) for t in slabs]
+    return slabs
+
+def solver_kernel(k_ref, shift_ref, rhs_ref, out_ref, m_ref):
+    nb = NB
+    ri = lax.broadcasted_iota(jnp.int32, (N, N), 0)
+    ci = lax.broadcasted_iota(jnp.int32, (N, N), 1)
+    m_ref[:, :N] = k_ref[...] + jnp.where(ri == ci, shift_ref[...], 0.0)
+    m_ref[:, N:] = jnp.zeros((N, 128), jnp.float32)
+    m_ref[:, N:N + 8] = rhs_ref[...]
+    steps = N // nb
+    tile = lambda k: (k * nb) // 128
+    slab = [m_ref[0:nb, 128 * t:128 * t + 128] for t in range(3)]
+    for k in range(steps):
+        t0, off = tile(k), (k * nb) % 128
+        diag = slab[t0]
+        cols = [jnp.broadcast_to(diag[:, off + q:off + q + 1], (nb, 128)) for q in range(nb)]
+        live = [t for t in range(3) if t == 2 or (t >= tile(k + 1) and k + 1 < steps)]
+        new = leaf(cols, [slab[t] for t in live], nb)
+        new = dict(zip(live, new))
+        wide = jnp.concatenate([new[t] for t in live], axis=1)
+        before, after = off, 128 - off - nb
+        pieces = ([jnp.zeros((before, 128 * len(live)), jnp.float32)] if before else []) + [wide] + (
+            [jnp.zeros((after, 128 * len(live)), jnp.float32)] if after else [])
+        padded = jnp.concatenate(pieces, axis=0)
+        lo = live[0] * 128
+        def update(r0, r1):
+            left = m_ref[r0:r1, 128 * t0:128 * t0 + 128]
+            return m_ref[r0:r1, lo:] - jnp.dot(left, padded, precision=HI, preferred_element_type=jnp.float32)
+        if k + 1 < steps:
+            nxt = update((k + 1) * nb, (k + 2) * nb)
+            for i, t in enumerate(live):
+                new[t] = nxt[:, 128 * i:128 * i + 128]
+            newslab = [new.get(t) for t in range(3)]
+            if k + 2 < steps:
+                m_ref[(k + 2) * nb:, lo:] = update((k + 2) * nb, N)
+        if k > 0:
+            m_ref[:k * nb, lo:] = update(0, k * nb)
+        m_ref[k * nb:(k + 1) * nb, lo:] = wide
+        if k + 1 < steps:
+            slab = newslab
+    out_ref[...] = m_ref[:, N:N + 8]
+
+def solve(k, shift, rhs):
+    return pl.pallas_call(
+        solver_kernel,
+        out_shape=jax.ShapeDtypeStruct((N, 8), jnp.float32),
+        in_specs=[pl.BlockSpec(memory_space=pltpu.VMEM)] * 3,
+        out_specs=pl.BlockSpec(memory_space=pltpu.VMEM),
+        scratch_shapes=[pltpu.VMEM((N, W), jnp.float32)],
+        name="solver",
+    )(k, shift, rhs)
 
 
 def passed_along(block, axis, distance):
@@ -81,27 +159,24 @@
         sources[0], local_inverse[0], preferred_element_type=jnp.float32
     ).astype(jnp.bfloat16)
     gradients = differences(snapshot_fields.astype(jnp.float32)).astype(jnp.bfloat16)
-    mass_weighted = (snapshot_fields[None] * (mass_weight * volume)[:, None, :]).astype(
-        jnp.bfloat16
-    )
-    mass_gram = jnp.einsum(
-        "csn,tn->cst", mass_weighted, snapshot_fields, preferred_element_type=jnp.float32
-    )
+    fields = snapshot_fields.astype(jnp.float32)
+    probed = jnp.dot(probe.T, fields, precision=HIGH_PRECISION)
+    loads = ((mass_weight * volume)[:, None, :] * probed).reshape(4 * NBASIS, NCELL)
+    corner_side = jnp.einsum("an,sn->as", loads, fields, precision=HIGH_PRECISION).reshape(4, NBASIS, SNAP)
     grad_weighted = (gradients[:, None] * (face_weight * volume)[:, :, None, :]).astype(
         jnp.bfloat16
     )
     stiffness = jnp.einsum(
         "dcsn,dtn->cst", grad_weighted, gradients, preferred_element_type=jnp.float32
     )
-    came_stiff, came_mass = passed_along((stiffness[1::2], mass_gram[1::2]), "sub", 1)
-    row_stiff = stiffness[0::2] + came_stiff
-    row_mass = mass_gram[0::2] + came_mass
-    below_stiff, below_mass = passed_along((row_stiff[1], row_mass[1]), "grp", 1)
-    node_stiff = row_stiff[0] + below_stiff
-    node_mass = row_mass[0] + below_mass
-    right_side = jnp.dot(node_mass, probe, precision=HIGH_PRECISION)
-    cholesky_factor = jnp.linalg.cholesky(node_stiff + jnp.diag(shift[0]))
-    coefficients = jax.scipy.linalg.cho_solve((cholesky_factor, True), right_side)
+    bf = jnp.bfloat16
+    came_stiff, came_side = passed_along((stiffness[1::2].astype(bf), corner_side[1::2]), "sub", 1)
+    row_stiff = stiffness[0::2] + came_stiff.astype(jnp.float32)
+    row_side = corner_side[0::2] + came_side
+    below_stiff, below_side = passed_along((row_stiff[1].astype(bf), row_side[1]), "grp", 1)
+    node_stiff = row_stiff[0] + below_stiff.astype(jnp.float32)
+    right_side = (row_side[0] + below_side).T
+    coefficients = solve(node_stiff, shift, right_side)
     own_coef = coefficients.astype(jnp.bfloat16)
     upper_coef = passed_along(own_coef, "grp", -1)
     right_coef, diagonal_coef = passed_along((own_coef, upper_coef), "sub", -1)

time: 153 us -> 82.6 us (0.54)
  other arithmetic: 68 us -> 8.06 us
  waiting for transfers between devices: 34.6 us -> 20.3 us
  Pallas kernels: 0 us -> 10.1 us
  starting transfers between devices: 18.1 us -> 25.1 us
  matrix products: 13.4 us -> 7.12 us
  local copies, waits for them, and re-layouts: 15.2 us -> 10.3 us
    another operation x12 -> x1, other arithmetic: 59.7 us -> 0.91 us  [local(): jnp.stack([own_coef, right_coef, upper_coef, diagonal_coef])]
    ppermute x7, waiting for transfers between devices: 34.6 us -> 20.3 us  [passed_along(): return lax.ppermute(block, axis, route)]
    pallas_call x0 -> x1, Pallas kernels: none -> 10.1 us  [solve(): pl.pallas_call(solver_kernel, out_shape=jax.ShapeDtypeStruct((N, 8), jnp....]
    ppermute x7, starting transfers between devices: 18.1 us -> 25.1 us  [passed_along(): return lax.ppermute(block, axis, route)]
    another operation x18 -> x4, local copies, waits for them, and re-layouts: 8 us -> 1.09 us  [local(): jnp.stack([own_coef, right_coef, upper_coef, diagonal_coef])]
    another operation x8 -> x0, matrix products: 5.64 us -> none  [the longest x6 2.87 us: local(): jax.scipy.linalg.cho_solve((cholesky_factor, True), right_side)]
    slice x6, local copies, waits for them, and re-layouts: 0.71 us -> 4.5 us  [differences(): jnp.roll(field, -stride, axis=-1) - field]
    another operation x1, other arithmetic: 0.46 us -> 2.42 us  [differences(): jnp.stack([jnp.roll(field, -stride, axis=-1) - field for stride in (CELLY...]
  transfers between devices with their start and end apart: 7 -> 7, of which waited for: 4 -> 5; matrix products, arithmetic and copies ran while one was open for 55% -> 7% of each run, Pallas kernels for 0% -> 0%
where the time goes in v1:
time: 82.6 us; the launch traced here: 82.1 us
  starting transfers between devices  25.1 us (30%)
  waiting for transfers between devices  20.3 us (25%)
  local copies, waits for them, and re-layouts  10.3 us (12%)
  Pallas kernels  10.1 us (12%)
  other arithmetic  8.06 us (10%)
  matrix products  7.12 us (9%)
  between operations  0.97 us (1%)
    ppermute x7, starting transfers between devices, passed_along(): return lax.ppermute(block, axis, route)  25.1 us
    ppermute x7, waiting for transfers between devices, passed_along(): return lax.ppermute(block, axis, route)  20.3 us
    pallas_call x1, Pallas kernels, solve(): pl.pallas_call(solver_kernel, out_shape=jax.ShapeDtypeStruct((N, 8), jnp....  10.1 us
    slice x6, local copies, waits for them, and re-layouts, differences(): jnp.roll(field, -stride, axis=-1) - field  4.5 us
    unnamed x9, local copies, waits for them, and re-layouts  3.35 us
    another operation x1, other arithmetic, differences(): jnp.stack([jnp.roll(field, -stride, axis=-1) - field for stride in (CELLY...  2.42 us
    dot_general x1, matrix products, local(): jnp.einsum('dcsn,dtn->cst', grad_weighted, gradients, preferred_element_t...  2.15 us
    dot_general x1, matrix products, local(): jnp.dot(sources[0], local_inverse[0], preferred_element_type=jnp.float32)  2.06 us
  transfers between devices with their start and end apart: 7, of which 5 were waited for; matrix products, arithmetic and copies ran while one was open for 7% of the time, Pallas kernels for 0%

profile of v1, /device:TPU:31, one launch (start us, length us, event | category | flops | bytes accessed | tf_op | source)
XLA Modules:
  0.0 82.1 jit_solution(6905925209108352700)
XLA Ops:
  0.6 1.7 %copy-done = bf16[1,1152,1152]{2,1,0:T(8,128)(2,1)S(1)} copy-done((bf16[1,1152,1152]{2,1,0:T(8,128)(2,1)S(1)}, bf16[1,1152,1152]{2,1,0:T(8,128)(2,1)}, u32[]{:S(2)}) %copy-start) | copy-done | bytes 2654232
  2.4 2.1 %fusion.5 = bf16[256,1152]{1,0:T(8,128)(2,1)S(1)} fusion(bf16[1,1152,1152]{2,1,0:T(8,128)(2,1)S(1)} %copy-done, bf16[1,256,1152]{2,1,0:T(8,128)(2,1)} %param.9), kind=kOutput, calls=%fused_computation.6 | convolution fusion | flops 679772160 | bytes 3833856 | tf_op jit(solution)/shard_map/dot_general | solution.py:158
  4.5 1.3 %slice.154 = f32[256,1056]{1,0:T(8,128)} slice(bf16[256,1152]{1,0:T(8,128)(2,1)S(1)} %fusion.5), slice={[0:256], [96:1152]} | slice | bytes 2162688 | tf_op jit(solution)/shard_map/jit(_roll_static)/slice | solution.py:151
  5.7 1.2 %slice.156 = f32[256,1144]{1,0:T(8,128)} slice(bf16[256,1152]{1,0:T(8,128)(2,1)S(1)} %fusion.5), slice={[0:256], [8:1152]} | slice | bytes 2342912 | tf_op jit(solution)/shard_map/jit(_roll_static)/slice | solution.py:151
  7.0 1.3 %slice.158 = f32[256,1151]{1,0:T(8,128)} slice(bf16[256,1152]{1,0:T(8,128)(2,1)S(1)} %fusion.5), slice={[0:256], [1:1152]} | slice | bytes 2357248 | tf_op jit(solution)/shard_map/jit(_roll_static)/slice | solution.py:151
  8.3 0.7 slice.159
  9.3 0.5 slice.169
  10.3 0.7 select_multiply_fusion.2
  11.3 2.4 %fusion.21 = (bf16[1,256,1152]{2,1,0:T(8,128)(2,1)S(1)}, bf16[1,256,1152]{2,1,0:T(8,128)(2,1)S(1)}, bf16[1,256,1152]{2,1,0:T(8,128)(2,1)S(1)}) fusion(bf16[256,1152]{1,0:T(8,128)(2,1)S(1)} %fusion.5, f32[256,96]{1,0:T(8,128)S(1)} %slice.155, f32[256,1056]{1,0:T(8,128)} %slice.154, f32[256,8]{1,0:T(8,128)S(1)} %slice.157, f32[256,1144]{1,0:T(8,128)} %slice.156, ...), kind=kLoop, calls=%fused_computation.25 | loop fusion | flops 2949120 | bytes 5898240 | tf_op jit(solution)/shard_map/stack | solution.py:150
  14.0 2.1 %fusion.72 = (bf16[4,256,256]{2,1,0:T(8,128)(2,1)S(1)}, f32[4,256,256]{2,1,0:T(8,128)S(1)}) fusion(bf16[1,256,1152]{2,1,0:T(8,128)(2,1)S(1)} %get-tuple-element.14, bf16[1,256,1152]{2,1,0:T(8,128)(2,1)S(1)} %get-tuple-element.13, bf16[1,256,1152]{2,1,0:T(8,128)(2,1)S(1)} %get-tuple-element.12, f32[3,4,1152]{2,0,1:T(4,128)S(1)} %copy.46, ...), kind=kOutput, calls=%fused_computation.145 | convolution fusion | flops 1821048832 | bytes 6936576 | tf_op jit(solution)/shard_map/dcsn,dtn->cst/dot_general | solution.py:169
  16.2 5.0 %collective-permute-start = (bf16[2,256,256]{2,1,0:T(8,128)(2,1)S(1)}, bf16[2,256,256]{2,1,0:T(8,128)(2,1)S(1)}, u32[]{:S(2)}, u32[]{:S(2)}) collective-permute-start(bf16[2,256,256]{2,1,0:T(8,128)(2,1)S(1)} %slice.141), channel_id=1, source_target_pairs={{31,0},{0,1},{1,2},{2,3},{3,4},{4,5},{5,6},{6,7},{7,8},{8,9},{9,10... | collective-permute-start | bytes 786440 | tf_op jit(solution)/shard_map/ppermute | solution.py:99
  21.5 1.2 %fusion.23 = f32[4,8,256]{1,2,0:T(8,128)S(1)} fusion(bf16[256,1152]{1,0:T(8,128)(2,1)S(1)} %fusion.5, f32[8,1152]{1,0:T(8,128)S(1)} %convolution_bitcast_fusion, f32[4,1152]{1,0:T(4,128)S(1)} %get-tuple-element.18), kind=kOutput, calls=%fused_computation.27 | convolution fusion | flops 113283072 | bytes 677888 | tf_op jit(solution)/shard_map/an,sn->as/dot_general | solution.py:165
  22.8 1.9 %collective-permute-start.2 = (f32[2,8,256]{1,2,0:T(8,128)S(1)}, f32[2,8,256]{1,2,0:T(8,128)S(1)}, u32[]{:S(2)}, u32[]{:S(2)}) collective-permute-start(f32[2,8,256]{1,2,0:T(8,128)S(1)} %slice.145), channel_id=1, source_target_pairs={{31,0},{0,1},{1,2},{2,3},{3,4},{4,5},{5,6},{6,7},{7,8},{8,9},{9,10... | collective-permute-start | bytes 49160 | tf_op jit(solution)/shard_map/ppermute | solution.py:99
  24.7 0.7 compare_select_fusion.2
  25.5 3.3 %collective-permute-done.2 = f32[2,8,256]{1,2,0:T(8,128)S(1)} collective-permute-done((f32[2,8,256]{1,2,0:T(8,128)S(1)}, f32[2,8,256]{1,2,0:T(8,128)S(1)}, u32[]{:S(2)}, u32[]{:S(2)}) %collective-permute-start.2) | collective-permute-done | bytes 16416 | tf_op jit(solution)/shard_map/ppermute | solution.py:99
  28.8 6.8 %collective-permute-start.3 = (f32[8,256]{0,1:T(8,128)S(1)}, f32[8,256]{0,1:T(8,128)S(1)}, u32[]{:S(2)}, u32[]{:S(2)}) collective-permute-start(f32[8,256]{0,1:T(8,128)S(1)} %slice_bitcast_fusion.4), channel_id=1, source_target_pairs={{480,0},{0,32},{32,64},{64,96},{96,128},{128,160},{160,192},{192,2... | collective-permute-start | bytes 24584 | tf_op jit(solution)/shard_map/ppermute | solution.py:99
  35.8 4.2 %collective-permute-start.1 = (bf16[256,256]{1,0:T(8,128)(2,1)S(1)}, bf16[256,256]{1,0:T(8,128)(2,1)S(1)}, u32[]{:S(2)}, u32[]{:S(2)}) collective-permute-start(bf16[256,256]{1,0:T(8,128)(2,1)S(1)} %fusion.34), channel_id=1, source_target_pairs={{480,0},{0,32},{32,64},{64,96},{96,128},{128,160},{160,192},{192,2... | collective-permute-start | bytes 393224 | tf_op jit(solution)/shard_map/ppermute | solution.py:99
  39.9 8.0 %collective-permute-done.3 = f32[8,256]{0,1:T(8,128)S(1)} collective-permute-done((f32[8,256]{0,1:T(8,128)S(1)}, f32[8,256]{0,1:T(8,128)S(1)}, u32[]{:S(2)}, u32[]{:S(2)}) %collective-permute-start.3) | collective-permute-done | bytes 8224 | tf_op jit(solution)/shard_map/ppermute | solution.py:99
  47.9 0.7 fusion.36.rhs_ref
  48.6 1.4 %collective-permute-done.1 = bf16[256,256]{1,0:T(8,128)(2,1)S(1)} collective-permute-done((bf16[256,256]{1,0:T(8,128)(2,1)S(1)}, bf16[256,256]{1,0:T(8,128)(2,1)S(1)}, u32[]{:S(2)}, u32[]{:S(2)}) %collective-permute-start.1) | collective-permute-done | bytes 131104 | tf_op jit(solution)/shard_map/ppermute | solution.py:99
  49.9 0.7 fusion.31.k_ref
  50.7 10.1 %solver.1 = f32[256,8]{1,0:T(8,128)} custom-call(f32[256,256]{1,0:T(8,128)} %fusion.31.k_ref, f32[1,256]{1,0:T(1,128)} %shift_ref.1, f32[256,8]{1,0:T(8,128)} %fusion.36.rhs_ref), custom_call_target="tpu_custom_call" | custom-call | tf_op jit(solution)/shard_map/solver/pallas_call | solution.py:86
  60.8 0.9 %convert_element_type.226 = bf16[256,8]{1,0:T(8,128)(2,1)S(1)} convert(f32[256,8]{1,0:T(8,128)} %solver.1) | non-fusion elementwise | flops 2048 | bytes 12288 | tf_op jit(solution)/shard_map/convert_element_type | solution.py:180
  61.7 3.4 %collective-permute-start.5 = (bf16[256,8]{1,0:T(8,128)(2,1)S(1)}, bf16[256,8]{1,0:T(8,128)(2,1)S(1)}, u32[]{:S(2)}, u32[]{:S(2)}) collective-permute-start(bf16[256,8]{1,0:T(8,128)(2,1)S(1)} %convert_element_type.226), channel_id=1, source_target_pairs={{32,0},{64,32},{96,64},{128,96},{160,128},{192,160},{224,192},{256... | collective-permute-start | bytes 12296 | tf_op jit(solution)/shard_map/ppermute | solution.py:99
  65.1 1.9 %collective-permute-start.4 = (bf16[256,8]{1,0:T(8,128)(2,1)S(1)}, bf16[256,8]{1,0:T(8,128)(2,1)S(1)}, u32[]{:S(2)}, u32[]{:S(2)}) collective-permute-start(bf16[256,8]{1,0:T(8,128)(2,1)S(1)} %convert_element_type.226), channel_id=1, source_target_pairs={{1,0},{2,1},{3,2},{4,3},{5,4},{6,5},{7,6},{8,7},{9,8},{10,9},{11,1... | collective-permute-start | bytes 12296 | tf_op jit(solution)/shard_map/ppermute | solution.py:99
  67.0 1.9 %collective-permute-start.6 = (bf16[256,8]{1,0:T(8,128)(2,1)S(1)}, bf16[256,8]{1,0:T(8,128)(2,1)}, u32[]{:S(2)}, u32[]{:S(2)}) collective-permute-start(bf16[256,8]{1,0:T(8,128)(2,1)S(1)} %collective-permute-done.5), channel_id=1, source_target_pairs={{1,0},{2,1},{3,2},{4,3},{5,4},{6,5},{7,6},{8,7},{9,8},{10,9},{11,1... | collective-permute-start | bytes 12296 | tf_op jit(solution)/shard_map/ppermute | solution.py:99
  69.0 0.9 %convert_bitcast_fusion = bf16[1,256,8]{2,1,0:T(8,128)(2,1)S(1)} fusion(f32[256,8]{1,0:T(8,128)} %solver.1), kind=kLoop, calls=%fused_computation.146 | loop fusion | flops 2048 | bytes 12288 | tf_op jit(solution)/shard_map/stack | solution.py:183
  69.9 1.6 %copy.54 = f32[1,256,8]{1,2,0:T(8,128)} copy(f32[1,256,8]{2,1,0:T(8,128)} %bitcast.111) | data formatting | bytes 16384
  71.5 5.6 %collective-permute-done.4 = bf16[256,8]{1,0:T(8,128)(2,1)S(1)} collective-permute-done((bf16[256,8]{1,0:T(8,128)(2,1)S(1)}, bf16[256,8]{1,0:T(8,128)(2,1)S(1)}, u32[]{:S(2)}, u32[]{:S(2)}) %collective-permute-start.4) | collective-permute-done | bytes 4128 | tf_op jit(solution)/shard_map/ppermute | solution.py:99
  77.3 2.1 %collective-permute-done.6 = bf16[256,8]{1,0:T(8,128)(2,1)} collective-permute-done((bf16[256,8]{1,0:T(8,128)(2,1)S(1)}, bf16[256,8]{1,0:T(8,128)(2,1)}, u32[]{:S(2)}, u32[]{:S(2)}) %collective-permute-start.6) | collective-permute-done | bytes 4128 | tf_op jit(solution)/shard_map/ppermute | solution.py:99
  79.4 0.9 %copy.52 = bf16[1,256,8]{1,2,0:T(8,128)(2,1)S(1)} copy(bf16[1,256,8]{2,1,0:T(8,128)(2,1)} %bitcast.29) | data formatting | bytes 8192 | tf_op jit(solution)/shard_map/stack | solution.py:183
  80.9 1.2 %fusion.16 = f32[1,32,32]{2,1,0:T(8,128)} fusion(f32[1,32,1152]{2,1,0:T(8,128)S(1)} %get-tuple-element.17, f32[1,32,1152]{2,1,0:T(8,128)S(1)} %get-tuple-element.16, f32[1,32,1152]{2,1,0:T(8,128)S(1)} %get-tuple-element.15, f32[3,1152]{1,0:T(4,128)S(1)} %pad_maximum_fusion.4), kind=kOutput, calls=%fused_computation.20 | convolution fusion | flops 43021312 | bytes 460288 | tf_op jit(solution)/shard_map/dan,dbn->ab/dot_general | solution.py:189
  (56 shorter events, 2.6 us)
Async XLA Ops:
  0.6 1.8 %copy-start = (bf16[1,1152,1152]{2,1,0:T(8,128)(2,1)S(1)}, bf16[1,1152,1152]{2,1,0:T(8,128)(2,1)}, u32[]{:S(2)}) copy-start(bf16[1,1152,1152]{2,1,0:T(8,128)(2,1)} %param.8) | copy-start | bytes 7962628
  7.0 2.0 %copy-start.2 = (s32[1,1152]{1,0:T(1,128)S(1)}, s32[1,1152]{1,0:T(1,128)}, u32[]{:S(2)}) copy-start(s32[1,1152]{1,0:T(1,128)} %param.6) | copy-start | bytes 13828
  7.0 2.0 %copy-start.3 = (f32[3]{0:T(128)S(1)}, f32[3]{0:T(128)}, u32[]{:S(2)}) copy-start(f32[3]{0:T(128)} %param.7) | copy-start | bytes 40
  14.0 7.2 %copy-start.1 = (f32[256,8]{0,1:T(8,128)S(1)}, f32[256,8]{0,1:T(8,128)}, u32[]{:S(2)}) copy-start(f32[256,8]{0,1:T(8,128)} %param.11) | copy-start | bytes 24580
  16.2 19.5 %collective-permute-start = (bf16[2,256,256]{2,1,0:T(8,128)(2,1)S(1)}, bf16[2,256,256]{2,1,0:T(8,128)(2,1)S(1)}, u32[]{:S(2)}, u32[]{:S(2)}) collective-permute-start(bf16[2,256,256]{2,1,0:T(8,128)(2,1)S(1)} %slice.141), channel_id=1, source_target_pairs={{31,0},{0,1},{1,2},{2,3},{3,4},{4,5},{5,6},{6,7},{7,8},{8,9},{9,10... | collective-permute-start | bytes 786440 | tf_op jit(solution)/shard_map/ppermute | solution.py:99
  22.8 6.0 %collective-permute-start.2 = (f32[2,8,256]{1,2,0:T(8,128)S(1)}, f32[2,8,256]{1,2,0:T(8,128)S(1)}, u32[]{:S(2)}, u32[]{:S(2)}) collective-permute-start(f32[2,8,256]{1,2,0:T(8,128)S(1)} %slice.145), channel_id=1, source_target_pairs={{31,0},{0,1},{1,2},{2,3},{3,4},{4,5},{5,6},{6,7},{7,8},{8,9},{9,10... | collective-permute-start | bytes 49160 | tf_op jit(solution)/shard_map/ppermute | solution.py:99
  28.8 19.1 %collective-permute-start.3 = (f32[8,256]{0,1:T(8,128)S(1)}, f32[8,256]{0,1:T(8,128)S(1)}, u32[]{:S(2)}, u32[]{:S(2)}) collective-permute-start(f32[8,256]{0,1:T(8,128)S(1)} %slice_bitcast_fusion.4), channel_id=1, source_target_pairs={{480,0},{0,32},{32,64},{64,96},{96,128},{128,160},{160,192},{192,2... | collective-permute-start | bytes 24584 | tf_op jit(solution)/shard_map/ppermute | solution.py:99
  35.8 14.2 %collective-permute-start.1 = (bf16[256,256]{1,0:T(8,128)(2,1)S(1)}, bf16[256,256]{1,0:T(8,128)(2,1)S(1)}, u32[]{:S(2)}, u32[]{:S(2)}) collective-permute-start(bf16[256,256]{1,0:T(8,128)(2,1)S(1)} %fusion.34), channel_id=1, source_target_pairs={{480,0},{0,32},{32,64},{64,96},{96,128},{128,160},{160,192},{192,2... | collective-permute-start | bytes 393224 | tf_op jit(solution)/shard_map/ppermute | solution.py:99
  61.7 5.3 %collective-permute-start.5 = (bf16[256,8]{1,0:T(8,128)(2,1)S(1)}, bf16[256,8]{1,0:T(8,128)(2,1)S(1)}, u32[]{:S(2)}, u32[]{:S(2)}) collective-permute-start(bf16[256,8]{1,0:T(8,128)(2,1)S(1)} %convert_element_type.226), channel_id=1, source_target_pairs={{32,0},{64,32},{96,64},{128,96},{160,128},{192,160},{224,192},{256... | collective-permute-start | bytes 12296 | tf_op jit(solution)/shard_map/ppermute | solution.py:99
  65.1 12.1 %collective-permute-start.4 = (bf16[256,8]{1,0:T(8,128)(2,1)S(1)}, bf16[256,8]{1,0:T(8,128)(2,1)S(1)}, u32[]{:S(2)}, u32[]{:S(2)}) collective-permute-start(bf16[256,8]{1,0:T(8,128)(2,1)S(1)} %convert_element_type.226), channel_id=1, source_target_pairs={{1,0},{2,1},{3,2},{4,3},{5,4},{6,5},{7,6},{8,7},{9,8},{10,9},{11,1... | collective-permute-start | bytes 12296 | tf_op jit(solution)/shard_map/ppermute | solution.py:99
  67.0 12.3 %collective-permute-start.6 = (bf16[256,8]{1,0:T(8,128)(2,1)S(1)}, bf16[256,8]{1,0:T(8,128)(2,1)}, u32[]{:S(2)}, u32[]{:S(2)}) collective-permute-start(bf16[256,8]{1,0:T(8,128)(2,1)S(1)} %collective-permute-done.5), channel_id=1, source_target_pairs={{1,0},{2,1},{3,2},{4,3},{5,4},{6,5},{7,6},{8,7},{9,8},{10,9},{11,1... | collective-permute-start | bytes 12296 | tf_op jit(solution)/shard_map/ppermute | solution.py:99

commit v2 on v1

v2 whole, which is shorter than its diff:
```python
import functools
import jax
import jax.numpy as jnp
from jax import lax
from jax.experimental import pallas as pl
from jax.experimental.pallas import tpu as pltpu
from jax.sharding import PartitionSpec as P

HI = lax.Precision.HIGHEST
N = 256
NB = 16
W = 384

def leaf(cols, slabs, nb):
    rows = lax.broadcasted_iota(jnp.int32, (nb, 128), 0)
    cols = list(cols)
    slabs = list(slabs)
    for p in range(0, nb, 2):
        c0, c1 = cols[p], cols[p + 1]
        a, b = c0[p:p + 1], c1[p:p + 1]
        bt, d = c0[p + 1:p + 2], c1[p + 1:p + 2]
        inv = 1.0 / (a * d - b * bt)
        a, b, bt, d = a * inv, b * inv, bt * inv, d * inv
        top, bottom = rows == p, rows == p + 1
        def step(t):
            r0, r1 = t[p:p + 1], t[p + 1:p + 2]
            s0 = d * r0 - b * r1
            s1 = a * r1 - bt * r0
            return jnp.where(top, s0, jnp.where(bottom, s1, t - c0 * s0 - c1 * s1))
        for q in range(p + 2, nb):
            cols[q] = step(cols[q])
        slabs = [step(t) for t in slabs]
    return slabs

def solver_kernel(k_ref, shift_ref, rhs_ref, out_ref, m_ref):
    nb = NB
    ri = lax.broadcasted_iota(jnp.int32, (N, N), 0)
    ci = lax.broadcasted_iota(jnp.int32, (N, N), 1)
    m_ref[:, :N] = k_ref[...] + jnp.where(ri == ci, shift_ref[...], 0.0)
    m_ref[:, N:] = jnp.zeros((N, 128), jnp.float32)
    m_ref[:, N:N + 8] = rhs_ref[...].T
    steps = N // nb
    tile = lambda k: (k * nb) // 128
    slab = [m_ref[0:nb, 128 * t:128 * t + 128] for t in range(3)]
    for k in range(steps):
        t0, off = tile(k), (k * nb) % 128
        diag = slab[t0]
        cols = [jnp.broadcast_to(diag[:, off + q:off + q + 1], (nb, 128)) for q in range(nb)]
        live = [t for t in range(3) if t == 2 or (t >= tile(k + 1) and k + 1 < steps)]
        new = leaf(cols, [slab[t] for t in live], nb)
        new = dict(zip(live, new))
        wide = jnp.concatenate([new[t] for t in live], axis=1)
        before, after = off, 128 - off - nb
        pieces = ([jnp.zeros((before, 128 * len(live)), jnp.float32)] if before else []) + [wide] + (
            [jnp.zeros((after, 128 * len(live)), jnp.float32)] if after else [])
        padded = jnp.concatenate(pieces, axis=0)
        lo = live[0] * 128
        def update(r0, r1):
            left = m_ref[r0:r1, 128 * t0:128 * t0 + 128]
            return m_ref[r0:r1, lo:] - jnp.dot(left, padded, precision=HI, preferred_element_type=jnp.float32)
        if k + 1 < steps:
            nxt = update((k + 1) * nb, (k + 2) * nb)
            for i, t in enumerate(live):
                new[t] = nxt[:, 128 * i:128 * i + 128]
            newslab = [new.get(t) for t in range(3)]
            if k + 2 < steps:
                m_ref[(k + 2) * nb:, lo:] = update((k + 2) * nb, N)
        if k > 0:
            m_ref[:k * nb, lo:] = update(0, k * nb)
        m_ref[k * nb:(k + 1) * nb, lo:] = wide
        if k + 1 < steps:
            slab = newslab
    out_ref[0] = m_ref[:, N:N + 8]

def solve(k, shift, rhs):
    return pl.pallas_call(
        solver_kernel,
        out_shape=jax.ShapeDtypeStruct((1, N, 8), jnp.float32),
        in_specs=[pl.BlockSpec(memory_space=pltpu.VMEM)] * 3,
        out_specs=pl.BlockSpec(memory_space=pltpu.VMEM),
        scratch_shapes=[pltpu.VMEM((N, W), jnp.float32)],
        name="solver",
    )(k, shift, rhs)


CELLX, CELLY, CELLZ, SNAP, NBASIS, PHASES, NCELL = 12, 12, 8, 256, 8, 3, 1152
STRIDES = (CELLY * CELLZ, CELLZ, 1)
CHUNKS = 3
PACK = 416
MESH = pl.DeviceIdType.MESH
NT = (((1,), (1,)), ((), ()))
VMEM = pl.BlockSpec(memory_space=pltpu.VMEM)
bf, f32 = jnp.bfloat16, jnp.float32


def ahead(field, stride):
    return pltpu.roll(field, NCELL - stride, axis=1)


def cell_weights():
    cell = lax.broadcasted_iota(jnp.int32, (1, NCELL), 1)
    run = lax.shift_right_logical(cell, 3)
    coord_x = lax.shift_right_logical(run * 683, 13)
    coord_y = run - coord_x * CELLY
    coord_z = lax.bitwise_and(cell, CELLZ - 1)
    fx = (coord_x.astype(f32) + 0.5) * (1.0 / CELLX)
    fy = (coord_y.astype(f32) + 0.5) * (1.0 / CELLY)
    partition = [(1.0 - fx) * (1.0 - fy), fx * (1.0 - fy), (1.0 - fx) * fy, fx * fy]
    inside = [coord_x < CELLX - 1, coord_y < CELLY - 1, coord_z < CELLZ - 1]
    return partition, inside


def permeability(labels_ref, perm_ref, inside):
    labels = labels_ref[...]
    kappa = jnp.where(labels == 0, perm_ref[0], jnp.where(labels == 1, perm_ref[1], perm_ref[2]))
    face = []
    for stride, keep in zip(STRIDES, inside):
        other = ahead(kappa, stride)
        face.append(jnp.where(keep, 2.0 * kappa * other / (kappa + other), 0.0))
    return kappa, face


def split3(x):
    hi = x.astype(bf)
    rest = x - hi.astype(f32)
    mid = rest.astype(bf)
    low = (rest - mid.astype(f32)).astype(bf)
    return jnp.concatenate([hi, mid, low], axis=0)


def neighbours(axes_size, step):
    grps, subs = axes_size
    g, s = lax.axis_index("grp"), lax.axis_index("sub")
    g1 = lax.rem(g + grps + step, grps)
    s1 = lax.rem(s + subs + step, subs)
    return [(g, s1), (g1, s), (g1, s1)]


def front_kernel(size, labels_ref, perm_ref, inverse_ref, sources_ref, probe_ref,
                 snap_ref, stiff_ref, side_ref, inv_ref, grad_ref, out_ref, in_ref,
                 load_sem, send_sem, recv_sem):
    rows = NCELL // CHUNKS
    loads = []
    for i in range(CHUNKS):
        part = pl.ds(i * rows, rows)
        loads.append(pltpu.make_async_copy(inverse_ref.at[0, part], inv_ref.at[part], load_sem.at[i]))
        loads[-1].start()
    onward, back = neighbours(size, 1), neighbours(size, -1)
    barrier = pltpu.get_barrier_semaphore()
    for device in onward + back:
        pl.semaphore_signal(barrier, inc=1, device_id=device, device_id_type=MESH)

    volume = 1.0 / NCELL
    partition, inside = cell_weights()
    kappa, face = permeability(labels_ref, perm_ref, inside)
    half = [f * (0.5 * volume) for f in face]
    weights = [jnp.concatenate([h * (p + ahead(p, s)) for h, s in zip(half, STRIDES)], axis=1).astype(bf)
               for p in partition]
    probe_rows = split3(probe_ref[...].T)

    total = None
    for i in range(CHUNKS):
        part = pl.ds(i * rows, rows)
        loads[i].wait()
        term = jnp.dot(sources_ref[0, :, part], inv_ref[part, :], preferred_element_type=f32)
        total = term if total is None else total + term
    snap_ref[...] = total.astype(bf)
    for r in range(0, SNAP, 64):
        field = snap_ref[r:r + 64, :].astype(f32)
        for d, stride in enumerate(STRIDES):
            grad_ref[r:r + 64, d * NCELL:(d + 1) * NCELL] = (ahead(field, stride) - field).astype(bf)

    def gram(corner):
        return lax.dot_general(grad_ref[...] * weights[corner], grad_ref[...], NT, preferred_element_type=f32)

    def triangle(g):
        return g[:128, :128], g[128:, :128], g[128:, 128:]

    probed = jnp.dot(probe_rows, snap_ref[...], preferred_element_type=f32)
    probed = probed[0:8] + probed[8:16] + probed[16:24]
    heavy = kappa * volume
    loads_ = jnp.concatenate([probed * (heavy * p) for p in partition], axis=0)
    side = lax.dot_general(split3(loads_), snap_ref[...], NT, preferred_element_type=f32)
    side = side[0:32] + side[32:64] + side[64:96]
    side = [side[8 * c:8 * c + 8] for c in range(4)]

    copies = []
    for slot, corner in ((2, 3), (1, 2), (0, 1)):
        for i, block in enumerate(triangle(gram(corner))):
            out_ref[slot, 128 * i:128 * i + 128, :] = block.astype(bf)
        hi = side[corner].astype(bf).astype(f32)
        low = side[corner] - hi
        out_ref[slot, 384:416, :] = jnp.concatenate(
            [hi[:, :128], hi[:, 128:], low[:, :128], low[:, 128:]], axis=0).astype(bf)
        copies.append(pltpu.make_async_remote_copy(
            src_ref=out_ref.at[slot], dst_ref=in_ref.at[slot], send_sem=send_sem.at[slot],
            recv_sem=recv_sem.at[slot], device_id=onward[slot], device_id_type=MESH))
        if slot == 2:
            pl.semaphore_wait(barrier, 6)
        copies[-1].start()

    own = list(triangle(gram(0)))
    own_side = side[0]
    for slot, copy in zip((2, 1, 0), copies):
        copy.wait_recv()
        for i in range(3):
            own[i] = own[i] + in_ref[slot, 128 * i:128 * i + 128, :].astype(f32)
        t = in_ref[slot, 384:416, :].astype(f32)
        own_side = own_side + jnp.concatenate([t[0:8] + t[16:24], t[8:16] + t[24:32]], axis=1)
    stiff_ref[:128, :128] = own[0]
    stiff_ref[128:, :128] = own[1]
    stiff_ref[:128, 128:] = own[1].T
    stiff_ref[128:, 128:] = own[2]
    side_ref[...] = own_side
    for copy in copies:
        copy.wait_send()


def front(size, labels, perm, inverse, sources, probe):
    return pl.pallas_call(
        functools.partial(front_kernel, size),
        out_shape=(jax.ShapeDtypeStruct((SNAP, NCELL), bf), jax.ShapeDtypeStruct((SNAP, SNAP), f32),
                   jax.ShapeDtypeStruct((NBASIS, SNAP), f32)),
        in_specs=[VMEM, pl.BlockSpec(memory_space=pltpu.SMEM), pl.BlockSpec(memory_space=pl.ANY), VMEM, VMEM],
        out_specs=(VMEM, VMEM, VMEM),
        scratch_shapes=[
            pltpu.VMEM((NCELL, NCELL), bf),
            pltpu.VMEM((SNAP, 3 * NCELL), bf),
            pltpu.VMEM((3, PACK, 128), bf),
            pltpu.VMEM((3, PACK, 128), bf),
            pltpu.SemaphoreType.DMA((CHUNKS,)),
            pltpu.SemaphoreType.DMA((3,)),
            pltpu.SemaphoreType.DMA((3,)),
        ],
        compiler_params=pltpu.CompilerParams(collective_id=0, has_side_effects=True),
        name="front",
    )(labels, perm, inverse, sources, probe)


def tail_kernel(size, labels_ref, perm_ref, snap_ref, coef_ref, element_ref, held_ref, send_ref, send_sem, recv_sem):
    onward, back = neighbours(size, 1), neighbours(size, -1)
    barrier = pltpu.get_barrier_semaphore()
    for device in onward + back:
        pl.semaphore_signal(barrier, inc=1, device_id=device, device_id_type=MESH)
    own = coef_ref[...].T.astype(bf).astype(f32)
    send_ref[...] = own
    pl.semaphore_wait(barrier, 6)
    copies = []
    for slot in (2, 1, 0):
        copies.append(pltpu.make_async_remote_copy(
            src_ref=send_ref, dst_ref=held_ref.at[slot], send_sem=send_sem.at[slot],
            recv_sem=recv_sem.at[slot], device_id=back[slot], device_id_type=MESH))
        copies[-1].start()
    partition, inside = cell_weights()
    kappa, face = permeability(labels_ref, perm_ref, inside)
    for copy in copies:
        copy.wait_recv()
    corners = jnp.concatenate([own, held_ref[0], held_ref[1], held_ref[2]], axis=0).astype(bf)
    field = jnp.dot(corners, snap_ref[...], preferred_element_type=f32)
    field = jnp.concatenate([field[8 * c:8 * c + 8] * partition[c] for c in range(4)], axis=0)
    slopes = [ahead(field, stride) - field for stride in STRIDES]
    left = jnp.concatenate([s * f for s, f in zip(slopes, face)], axis=1)
    right = jnp.concatenate(slopes, axis=1)
    element = lax.dot_general(left, right, NT, precision=HI, preferred_element_type=f32)
    element_ref[0] = element * (1.0 / (NCELL * SNAP))
    for copy in copies:
        copy.wait_send()


def tail(size, labels, perm, snap, coef):
    return pl.pallas_call(
        functools.partial(tail_kernel, size),
        out_shape=jax.ShapeDtypeStruct((1, 32, 32), f32),
        in_specs=[VMEM, pl.BlockSpec(memory_space=pltpu.SMEM), VMEM, VMEM],
        out_specs=VMEM,
        scratch_shapes=[
            pltpu.VMEM((3, NBASIS, SNAP), f32),
            pltpu.VMEM((NBASIS, SNAP), f32),
            pltpu.SemaphoreType.DMA((3,)),
            pltpu.SemaphoreType.DMA((3,)),
        ],
        compiler_params=pltpu.CompilerParams(collective_id=1, has_side_effects=True),
        name="tail",
    )(labels, perm, snap, coef)


def local(size, phase_labels, phase_perm, local_inverse, sources, shift, probe):
    snap, stiff, side = front(size, phase_labels, phase_perm, local_inverse, sources, probe)
    coefficients = solve(stiff, shift, side)
    element_stiffness = tail(size, phase_labels, phase_perm, snap, coefficients[0])
    return (coefficients, element_stiffness)


def solution(mesh):
    size = (mesh.shape["grp"], mesh.shape["sub"])
    in_specs = (
        P(("grp", "sub"), None),
        P(),
        P(("grp", "sub"), None, None),
        P(("grp", "sub"), None, None),
        P(("grp", "sub"), None),
        P(),
    )
    out_specs = (P(("grp", "sub"), None, None), P(("grp", "sub"), None, None))
    return jax.shard_map(functools.partial(local, size), mesh=mesh, in_specs=in_specs, out_specs=out_specs, check_vma=False)
```

time: 82.6 us -> 52.5 us (0.64)
  the two profiles are of different devices: /device:TPU:31 before, /device:TPU:63 now
where the time goes in v2:
time: 52.5 us; the launch traced here: 52.2 us
  Pallas kernels  47.1 us (90%)
  local copies, waits for them, and re-layouts  4.37 us (8%)
  between operations  0.65 us (1%)
    pallas_call x1, Pallas kernels, front(): pl.pallas_call(functools.partial(front_kernel, size), out_shape=(jax.Shap...  23.9 us
    pallas_call x1, Pallas kernels, tail(): pl.pallas_call(functools.partial(tail_kernel, size), out_shape=jax.ShapeD...  13.1 us
    pallas_call x1, Pallas kernels, solve(): pl.pallas_call(solver_kernel, out_shape=jax.ShapeDtypeStruct((1, N, 8), j...  10.1 us
    unnamed x3, local copies, waits for them, and re-layouts  4.37 us

profile of v2, /device:TPU:63, one launch (start us, length us, event | category | flops | bytes accessed | tf_op | source)
XLA Modules:
  0.0 52.2 jit_solution(3281006204783528896)
XLA Ops:
  0.6 1.5 %copy.8.probe_ref = f32[256,8]{1,0:T(8,128)} copy(f32[256,8]{0,1:T(8,128)} %param.11) | data formatting | bytes 16384 | tf_op args[5]
  2.1 23.9 %front.1 = (bf16[256,1152]{1,0:T(8,128)(2,1)}, f32[256,256]{1,0:T(8,128)}, f32[8,256]{1,0:T(8,128)}) custom-call(s32[1,1152]{1,0:T(1,128)} %labels_ref.3, f32[3]{0:T(128)} %perm_ref.3, bf16[1,1152,1152]{2,1,0:T(8,128)(2,1)} %inverse_ref.1, bf16[1,256,1152]{2,1,0:T(8,128)(2,1)} %sources_ref.1, f32[256,8]{1,0:T(8,128)} %copy.8.probe_ref), custom_call_target="tpu_custom_call" | custom-call | tf_op jit(solution)/shard_map/front/pallas_call | solution.py:220
  26.0 10.1 %solver.1 = f32[1,256,8]{2,1,0:T(8,128)} custom-call(f32[256,256]{1,0:T(8,128)} %get-tuple-element.5.k_ref, f32[1,256]{1,0:T(1,128)} %shift_ref.1, f32[8,256]{1,0:T(8,128)} %get-tuple-element.6.rhs_ref), custom_call_target="tpu_custom_call" | custom-call | tf_op jit(solution)/shard_map/solver/pallas_call | solution.py:76
  36.1 13.1 %tail.1 = f32[1,32,32]{2,1,0:T(8,128)} custom-call(s32[1,1152]{1,0:T(1,128)} %labels_ref.3, f32[3]{0:T(128)} %perm_ref.3, bf16[256,1152]{1,0:T(8,128)(2,1)} %get-tuple-element.7.snap_ref, f32[256,8]{1,0:T(8,128)} %bitcast.1), custom_call_target="tpu_custom_call" | custom-call | tf_op jit(solution)/shard_map/tail/pallas_call | solution.py:271
  49.3 1.6 %copy.9 = f32[1,256,8]{1,2,0:T(8,128)} copy(f32[1,256,8]{2,1,0:T(8,128)} %solver.1) | data formatting | bytes 16384
  50.8 1.3 %copy.11 = f32[1,32,32]{2,1,0:T(8,128)} copy(f32[1,32,32]{2,1,0:T(8,128)} %tail.1) | data formatting | bytes 8192

commit v3 on v2

v3 whole, which is shorter than its diff:
```python
import functools
import jax
import jax.numpy as jnp
from jax import lax
from jax.experimental import pallas as pl
from jax.experimental.pallas import tpu as pltpu
from jax.sharding import PartitionSpec as P

HI = lax.Precision.HIGHEST
N = 256
NB = 16
W = 384
bf, f32 = jnp.bfloat16, jnp.float32


def spread(group, row):
    return jnp.broadcast_to(group[row:row + 1], (8, 128))


def leaf(cols, slabs):
    row = lax.broadcasted_iota(jnp.int32, (8, 128), 0)
    cols, slabs = list(cols), list(slabs)
    for p in range(0, NB, 2):
        g, i = p // 8, p % 8
        c0, c1 = cols[p], cols[p + 1]
        a, b = spread(c0[g], i), spread(c1[g], i)
        bt, d = spread(c0[g], i + 1), spread(c1[g], i + 1)
        inv = 1.0 / (a * d - b * bt)
        a, b, bt, d = a * inv, b * inv, bt * inv, d * inv
        e0 = [x * d - y * bt for x, y in zip(c0, c1)]
        e1 = [y * a - x * b for x, y in zip(c0, c1)]
        first, second = row == i, row == i + 1
        e0[g] = jnp.where(first, -d, jnp.where(second, bt, e0[g]))
        e1[g] = jnp.where(first, b, jnp.where(second, -a, e1[g]))
        pair = (row == i) | (row == i + 1)

        def step(t):
            r0, r1 = spread(t[g], i), spread(t[g], i + 1)
            z = list(t)
            z[g] = jnp.where(pair, 0.0, t[g])
            return [x - u * r0 - v * r1 for x, u, v in zip(z, e0, e1)]

        for q in range(p + 2, NB):
            cols[q] = step(cols[q])
        slabs = [step(t) for t in slabs]
    return slabs


def halves(x):
    hi = x.astype(bf)
    return hi, (x - hi.astype(f32)).astype(bf)


def column(tile, off, q):
    return [jnp.broadcast_to(t[:, off + q:off + q + 1], (8, 128)) for t in tile]


def eliminate(m_ref):
    steps = N // NB
    tile = lambda k: (k * NB) // 128

    def read(k, t):
        return [m_ref[k * NB + 8 * g:k * NB + 8 * g + 8, 128 * t:128 * t + 128] for g in range(2)]

    slab = {t: read(0, t) for t in range(3)}
    for k in range(steps):
        t0, off = tile(k), (k * NB) % 128
        cols = [column(slab[t0], off, q) for q in range(NB)]
        live = [t for t in range(3) if t == 2 or (t >= tile(k + 1) and k + 1 < steps)]
        new = dict(zip(live, leaf(cols, [slab[t] for t in live])))
        if k + 1 < steps:
            factor_tile = read(k + 1, t0)
            factors = [column(factor_tile, off, q) for q in range(NB)]
            nxt = {}
            for t in live:
                rows = [spread(new[t][q // 8], q % 8) for q in range(NB)]
                groups = []
                for g, start in enumerate(read(k + 1, t)):
                    parts = []
                    for c in range(0, NB, 4):
                        s = factors[c][g] * rows[c]
                        for q in range(c + 1, c + 4):
                            s = s + factors[q][g] * rows[q]
                        parts.append(s)
                    groups.append(start - ((parts[0] + parts[1]) + (parts[2] + parts[3])))
                nxt[t] = groups
        wide = jnp.concatenate([jnp.concatenate(new[t], axis=0) for t in live], axis=1)
        hi, low = halves(wide)
        width = 128 * len(live)
        gap = lambda n: [jnp.zeros((n, width), bf)] if n else []
        right = jnp.concatenate(
            [piece for x in (hi, hi, low, low) for piece in gap(off) + [x] + gap(128 - off - NB)], axis=0)
        lo = live[0] * 128

        def update(r0, r1):
            if r1 <= r0:
                return
            lhi, llow = halves(m_ref[r0:r1, 128 * t0:128 * t0 + 128])
            left = jnp.concatenate([lhi, llow, lhi, llow], axis=1)
            m_ref[r0:r1, lo:] = m_ref[r0:r1, lo:] - jnp.dot(left, right, preferred_element_type=f32)

        update((k + 2) * NB, N)
        update(0, k * NB)
        m_ref[k * NB:(k + 1) * NB, lo:] = wide
        if k + 1 < steps:
            slab = nxt


CELLX, CELLY, CELLZ, SNAP, NBASIS, PHASES, NCELL = 12, 12, 8, 256, 8, 3, 1152
STRIDES = (CELLY * CELLZ, CELLZ, 1)
CHUNKS = 3
PACK = 304
MESH = pl.DeviceIdType.MESH
NT = (((1,), (1,)), ((), ()))
VMEM = pl.BlockSpec(memory_space=pltpu.VMEM)


def ahead(field, stride):
    return pltpu.roll(field, NCELL - stride, axis=1)


def cell_weights():
    cell = lax.broadcasted_iota(jnp.int32, (1, NCELL), 1)
    run = lax.shift_right_logical(cell, 3)
    coord_x = lax.shift_right_logical(run * 683, 13)
    coord_y = run - coord_x * CELLY
    coord_z = lax.bitwise_and(cell, CELLZ - 1)
    fx = (coord_x.astype(f32) + 0.5) * (1.0 / CELLX)
    fy = (coord_y.astype(f32) + 0.5) * (1.0 / CELLY)
    partition = [(1.0 - fx) * (1.0 - fy), fx * (1.0 - fy), (1.0 - fx) * fy, fx * fy]
    inside = [coord_x < CELLX - 1, coord_y < CELLY - 1, coord_z < CELLZ - 1]
    return partition, inside


def permeability(labels_ref, perm_ref, inside):
    labels = labels_ref[...]
    kappa = jnp.where(labels == 0, perm_ref[0], jnp.where(labels == 1, perm_ref[1], perm_ref[2]))
    face = []
    for stride, keep in zip(STRIDES, inside):
        other = ahead(kappa, stride)
        face.append(jnp.where(keep, 2.0 * kappa * other / (kappa + other), 0.0))
    return kappa, face


def split3(x):
    hi = x.astype(bf)
    rest = x - hi.astype(f32)
    mid = rest.astype(bf)
    low = (rest - mid.astype(f32)).astype(bf)
    return jnp.concatenate([hi, mid, low], axis=0)


def neighbours(axes_size, step):
    grps, subs = axes_size
    g, s = lax.axis_index("grp"), lax.axis_index("sub")
    g1 = lax.rem(g + grps + step, grps)
    s1 = lax.rem(s + subs + step, subs)
    return [(g, s1), (g1, s), (g1, s1)]


def basis_kernel(size, labels_ref, perm_ref, inverse_ref, sources_ref, shift_ref, probe_ref,
                 coef_ref, element_ref, inv_ref, src_ref, snap_ref, grad_ref, out_ref, in_ref, m_ref,
                 coef_out_ref, coef_in_ref, load_sem, send_sem, recv_sem, coef_send_sem, coef_recv_sem):
    rows = NCELL // CHUNKS
    loads = []
    for i in range(CHUNKS):
        part = pl.ds(i * rows, rows)
        loads.append((
            pltpu.make_async_copy(sources_ref.at[0, :, part], src_ref.at[:, part], load_sem.at[0, i]),
            pltpu.make_async_copy(inverse_ref.at[0, part], inv_ref.at[part], load_sem.at[1, i])))
        for load in loads[-1]:
            load.start()
    onward, back = neighbours(size, 1), neighbours(size, -1)
    barrier = pltpu.get_barrier_semaphore()
    for device in onward + back:
        pl.semaphore_signal(barrier, inc=1, device_id=device, device_id_type=MESH)

    volume = 1.0 / NCELL
    partition, inside = cell_weights()
    kappa, face = permeability(labels_ref, perm_ref, inside)
    half = [f * (0.5 * volume) for f in face]
    weights = [jnp.concatenate([h * (p + ahead(p, s)) for h, s in zip(half, STRIDES)], axis=1).astype(bf)
               for p in partition]
    probe_rows = split3(probe_ref[...])

    total = None
    for i in range(CHUNKS):
        part = pl.ds(i * rows, rows)
        for load in loads[i]:
            load.wait()
        term = jnp.dot(src_ref[:, part], inv_ref[part, :], preferred_element_type=f32)
        total = term if total is None else total + term
    snap_ref[...] = total.astype(bf)
    for r in range(0, SNAP, 64):
        field = snap_ref[r:r + 64, :].astype(f32)
        for d, stride in enumerate(STRIDES):
            grad_ref[r:r + 64, d * NCELL:(d + 1) * NCELL] = (ahead(field, stride) - field).astype(bf)

    row = lax.broadcasted_iota(jnp.int32, (128, 128), 0)
    col = lax.broadcasted_iota(jnp.int32, (128, 128), 1)

    def gram(corner):
        g = lax.dot_general(grad_ref[...] * weights[corner], grad_ref[...], NT, preferred_element_type=f32)
        first, below, second = g[:128, :128], g[128:, :128], g[128:, 128:]
        diagonal = jnp.sum(jnp.where(row == col, second, 0.0), axis=0, keepdims=True)
        return [jnp.where(row >= col, first, second), below, diagonal]

    probed = jnp.dot(probe_rows, snap_ref[...], preferred_element_type=f32)
    probed = probed[0:8] + probed[8:16] + probed[16:24]
    heavy = kappa * volume
    loaded = jnp.concatenate([probed * (heavy * p) for p in partition], axis=0)
    side = lax.dot_general(split3(loaded), snap_ref[...], NT, preferred_element_type=f32)
    side = side[0:32] + side[32:64] + side[64:96]
    side = [side[8 * c:8 * c + 8] for c in range(4)]

    copies = {}
    for slot, corner in ((2, 3), (1, 2), (0, 1)):
        square, below, diagonal = gram(corner)
        hi = side[corner].astype(bf).astype(f32)
        low = side[corner] - hi
        out_ref[slot, 0:128, :] = square.astype(bf)
        out_ref[slot, 128:256, :] = below.astype(bf)
        out_ref[slot, 256:288, :] = jnp.concatenate(
            [hi[:, :128], hi[:, 128:], low[:, :128], low[:, 128:]], axis=0).astype(bf)
        out_ref[slot, 288:304, :] = jnp.broadcast_to(diagonal, (16, 128)).astype(bf)
        copies[slot] = pltpu.make_async_remote_copy(
            src_ref=out_ref.at[slot], dst_ref=in_ref.at[slot], send_sem=send_sem.at[slot],
            recv_sem=recv_sem.at[slot], device_id=onward[slot], device_id_type=MESH)
        if slot == 2:
            pl.semaphore_wait(barrier, 6)
        copies[slot].start()

    square, below, diagonal = gram(0)
    own_side = side[0]
    for slot in (0, 1, 2):
        copies[slot].wait_recv()
        square = square + in_ref[slot, 0:128, :].astype(f32)
        below = below + in_ref[slot, 128:256, :].astype(f32)
        t = in_ref[slot, 256:288, :].astype(f32)
        own_side = own_side + jnp.concatenate([t[0:8] + t[16:24], t[8:16] + t[24:32]], axis=1)
        diagonal = diagonal + in_ref[slot, 288:304, :].astype(f32)[0:1]
    turned = square.T
    shift = shift_ref[...]
    m_ref[:128, :128] = jnp.where(row >= col, square, turned) + jnp.where(row == col, shift[:, :128], 0.0)
    m_ref[128:, :128] = below
    m_ref[:128, 128:256] = below.T
    m_ref[128:, 128:256] = jnp.where(
        row == col, diagonal + shift[:, 128:], jnp.where(row < col, square, turned))
    m_ref[:, N:] = jnp.concatenate([own_side, jnp.zeros((120, SNAP), f32)], axis=0).T
    eliminate(m_ref)

    solved = m_ref[:, N:].T[0:8]
    coef_ref[0] = solved
    own = solved.astype(bf).astype(f32)
    coef_out_ref[...] = own
    sends = []
    for slot in (2, 1, 0):
        sends.append(pltpu.make_async_remote_copy(
            src_ref=coef_out_ref, dst_ref=coef_in_ref.at[slot], send_sem=coef_send_sem.at[slot],
            recv_sem=coef_recv_sem.at[slot], device_id=back[slot], device_id_type=MESH))
        sends[-1].start()
    for send in sends:
        send.wait_recv()
    corners = jnp.concatenate([own, coef_in_ref[0], coef_in_ref[1], coef_in_ref[2]], axis=0).astype(bf)
    field = jnp.dot(corners, snap_ref[...], preferred_element_type=f32)
    field = jnp.concatenate([field[8 * c:8 * c + 8] * partition[c] for c in range(4)], axis=0)
    slopes = [ahead(field, stride) - field for stride in STRIDES]
    left = jnp.concatenate([s * f for s, f in zip(slopes, face)], axis=1)
    right = jnp.concatenate(slopes, axis=1)
    element_ref[0] = lax.dot_general(left, right, NT, precision=HI, preferred_element_type=f32)
    for slot in copies:
        copies[slot].wait_send()
    for send in sends:
        send.wait_send()


def scale_kernel(coef_ref, element_ref, coef_out_ref, element_out_ref):
    coef_out_ref[...] = coef_ref[...]
    element_out_ref[...] = element_ref[...] * (1.0 / (NCELL * SNAP))


def local(size, phase_labels, phase_perm, local_inverse, sources, shift, probe):
    shapes = (jax.ShapeDtypeStruct((1, NBASIS, SNAP), f32), jax.ShapeDtypeStruct((1, 32, 32), f32))
    coef, element = pl.pallas_call(
        functools.partial(basis_kernel, size),
        out_shape=shapes,
        in_specs=[VMEM, pl.BlockSpec(memory_space=pltpu.SMEM), pl.BlockSpec(memory_space=pl.ANY),
                  pl.BlockSpec(memory_space=pl.ANY), VMEM, VMEM],
        out_specs=(VMEM, VMEM),
        scratch_shapes=[
            pltpu.VMEM((NCELL, NCELL), bf),
            pltpu.VMEM((SNAP, NCELL), bf),
            pltpu.VMEM((SNAP, NCELL), bf),
            pltpu.VMEM((SNAP, 3 * NCELL), bf),
            pltpu.VMEM((3, PACK, 128), bf),
            pltpu.VMEM((3, PACK, 128), bf),
            pltpu.VMEM((N, W), f32),
            pltpu.VMEM((NBASIS, SNAP), f32),
            pltpu.VMEM((3, NBASIS, SNAP), f32),
            pltpu.SemaphoreType.DMA((2, CHUNKS)),
            pltpu.SemaphoreType.DMA((3,)),
            pltpu.SemaphoreType.DMA((3,)),
            pltpu.SemaphoreType.DMA((3,)),
            pltpu.SemaphoreType.DMA((3,)),
        ],
        compiler_params=pltpu.CompilerParams(collective_id=0, has_side_effects=True),
        name="basis",
    )(phase_labels, phase_perm, local_inverse, sources, shift, probe.T)
    coef, element = pl.pallas_call(
        scale_kernel, out_shape=shapes, in_specs=[VMEM, VMEM], out_specs=(VMEM, VMEM), name="scale",
    )(coef, element)
    return (coef.transpose(0, 2, 1), element)


def solution(mesh):
    size = (mesh.shape["grp"], mesh.shape["sub"])
    in_specs = (
        P(("grp", "sub"), None),
        P(),
        P(("grp", "sub"), None, None),
        P(("grp", "sub"), None, None),
        P(("grp", "sub"), None),
        P(),
    )
    out_specs = (P(("grp", "sub"), None, None), P(("grp", "sub"), None, None))
    return jax.shard_map(functools.partial(local, size), mesh=mesh, in_specs=in_specs, out_specs=out_specs, check_vma=False)
```

time: 52.5 us -> 35.8 us (0.68)
  the two profiles are of different devices: /device:TPU:63 before, /device:TPU:31 now
where the time goes in v3:
time: 35.8 us; the launch traced here: 35.5 us
  Pallas kernels  34.9 us (97%)
  between operations  0.64 us (2%)
    pallas_call x1, Pallas kernels, local(): pl.pallas_call(functools.partial(basis_kernel, size), out_shape=shapes, i...  33.6 us
    pallas_call x1, Pallas kernels, local(): pl.pallas_call(scale_kernel, out_shape=shapes, in_specs=[VMEM, VMEM], out...  1.35 us

profile of v3, /device:TPU:31, one launch (start us, length us, event | category | flops | bytes accessed | tf_op | source)
XLA Modules:
  0.0 35.5 jit_solution(13355442614479959161)
XLA Ops:
  0.6 33.6 %basis.1 = (f32[1,8,256]{2,1,0:T(8,128)}, f32[1,32,32]{2,1,0:T(8,128)}) custom-call(s32[1,1152]{1,0:T(1,128)} %labels_ref.1, f32[3]{0:T(128)} %perm_ref.1, bf16[1,1152,1152]{2,1,0:T(8,128)(2,1)} %inverse_ref.1, bf16[1,256,1152]{2,1,0:T(8,128)(2,1)} %sources_ref.1, f32[1,256]{1,0:T(1,128)} %shift_ref.1, f32[8,256]{1,0:T(8,128)} %bitcast.2), custom_call_target="tpu_custom_call" | custom-call | tf_op jit(solution)/shard_map/basis/pallas_call | solution.py:284
  34.2 1.3 %scale.1 = (f32[1,8,256]{2,1,0:T(8,128)}, f32[1,32,32]{2,1,0:T(8,128)}) custom-call(f32[1,8,256]{2,1,0:T(8,128)} %get-tuple-element.6.coef_ref, f32[1,32,32]{2,1,0:T(8,128)} %get-tuple-element.7.element_ref), custom_call_target="tpu_custom_call" | custom-call | tf_op jit(solution)/shard_map/scale/pallas_call | solution.py:309

commit v4 on v3

--- a/solution.py
+++ b/solution.py
@@ -10,6 +10,7 @@
 N = 256
 NB = 16
 W = 384
+NBASIS = 8
 bf, f32 = jnp.bfloat16, jnp.float32
 
 
@@ -58,6 +59,14 @@
 def eliminate(m_ref):
     steps = N // NB
     tile = lambda k: (k * NB) // 128
+    low8 = lambda rows: lax.broadcasted_iota(jnp.int32, (rows, 128), 1) < NBASIS
+
+    def moved(k, pieces):
+        if k == 0:
+            return {0: jnp.where(low8(pieces[0].shape[0]), pieces[2], pieces[0]), 1: pieces[1]}
+        if k == 8:
+            return {1: jnp.where(low8(pieces[1].shape[0]), pieces[0], pieces[1])}
+        return pieces
 
     def read(k, t):
         return [m_ref[k * NB + 8 * g:k * NB + 8 * g + 8, 128 * t:128 * t + 128] for g in range(2)]
@@ -66,7 +75,7 @@
     for k in range(steps):
         t0, off = tile(k), (k * NB) % 128
         cols = [column(slab[t0], off, q) for q in range(NB)]
-        live = [t for t in range(3) if t == 2 or (t >= tile(k + 1) and k + 1 < steps)]
+        live = [0, 1, 2] if k == 0 else [0, 1] if k <= 8 else [1]
         new = dict(zip(live, leaf(cols, [slab[t] for t in live])))
         if k + 1 < steps:
             factor_tile = read(k + 1, t0)
@@ -84,8 +93,10 @@
                         parts.append(s)
                     groups.append(start - ((parts[0] + parts[1]) + (parts[2] + parts[3])))
                 nxt[t] = groups
-        wide = jnp.concatenate([jnp.concatenate(new[t], axis=0) for t in live], axis=1)
-        hi, low = halves(wide)
+            both = [moved(k, {t: nxt[t][g] for t in live}) for g in range(2)]
+            slab = {t: [both[0][t], both[1][t]] for t in both[0]}
+        new = {t: jnp.concatenate(new[t], axis=0) for t in live}
+        hi, low = halves(jnp.concatenate([new[t] for t in live], axis=1))
         width = 128 * len(live)
         gap = lambda n: [jnp.zeros((n, width), bf)] if n else []
         right = jnp.concatenate(
@@ -97,19 +108,22 @@
                 return
             lhi, llow = halves(m_ref[r0:r1, 128 * t0:128 * t0 + 128])
             left = jnp.concatenate([lhi, llow, lhi, llow], axis=1)
-            m_ref[r0:r1, lo:] = m_ref[r0:r1, lo:] - jnp.dot(left, right, preferred_element_type=f32)
+            got = m_ref[r0:r1, lo:lo + width] - jnp.dot(left, right, preferred_element_type=f32)
+            pieces = moved(k, {t: got[:, 128 * i:128 * i + 128] for i, t in enumerate(live)})
+            for t in pieces:
+                m_ref[r0:r1, 128 * t:128 * t + 128] = pieces[t]
 
         update((k + 2) * NB, N)
         update(0, k * NB)
-        m_ref[k * NB:(k + 1) * NB, lo:] = wide
-        if k + 1 < steps:
-            slab = nxt
+        pieces = moved(k, new)
+        for t in pieces:
+            m_ref[k * NB:(k + 1) * NB, 128 * t:128 * t + 128] = pieces[t]
 
 
 CELLX, CELLY, CELLZ, SNAP, NBASIS, PHASES, NCELL = 12, 12, 8, 256, 8, 3, 1152
 STRIDES = (CELLY * CELLZ, CELLZ, 1)
-CHUNKS = 3
-PACK = 304
+CHUNKS = ((0, 256), (256, 768), (768, 1152))
+PACK = 272
 MESH = pl.DeviceIdType.MESH
 NT = (((1,), (1,)), ((), ()))
 VMEM = pl.BlockSpec(memory_space=pltpu.VMEM)
@@ -133,8 +147,8 @@
 
 
 def permeability(labels_ref, perm_ref, inside):
-    labels = labels_ref[...]
-    kappa = jnp.where(labels == 0, perm_ref[0], jnp.where(labels == 1, perm_ref[1], perm_ref[2]))
+    labels, perm = labels_ref[...], perm_ref[...]
+    kappa = jnp.where(labels == 0, perm[:, 0:1], jnp.where(labels == 1, perm[:, 1:2], perm[:, 2:3]))
     face = []
     for stride, keep in zip(STRIDES, inside):
         other = ahead(kappa, stride)
@@ -158,39 +172,38 @@
     return [(g, s1), (g1, s), (g1, s1)]
 
 
-def basis_kernel(size, labels_ref, perm_ref, inverse_ref, sources_ref, shift_ref, probe_ref,
-                 coef_ref, element_ref, inv_ref, src_ref, snap_ref, grad_ref, out_ref, in_ref, m_ref,
-                 coef_out_ref, coef_in_ref, load_sem, send_sem, recv_sem, coef_send_sem, coef_recv_sem):
-    rows = NCELL // CHUNKS
-    loads = []
-    for i in range(CHUNKS):
-        part = pl.ds(i * rows, rows)
-        loads.append((
-            pltpu.make_async_copy(sources_ref.at[0, :, part], src_ref.at[:, part], load_sem.at[0, i]),
-            pltpu.make_async_copy(inverse_ref.at[0, part], inv_ref.at[part], load_sem.at[1, i])))
-        for load in loads[-1]:
-            load.start()
+def basis_kernel(size, labels_hbm, perm_hbm, inverse_ref, sources_ref, shift_hbm, probe_hbm,
+                 coef_ref, element_ref, labels_ref, perm_ref, shift_ref, probe_ref, inv_ref, src_ref, snap_ref,
+                 grad_ref, out_ref, in_ref, side_out_ref, side_in_ref, m_ref, coef_out_ref, coef_in_ref,
+                 small_sem, load_sem, send_sem, recv_sem, side_send_sem, side_recv_sem, coef_send_sem, coef_recv_sem):
     onward, back = neighbours(size, 1), neighbours(size, -1)
+    loads = [pltpu.make_async_copy(sources_ref.at[0], src_ref, load_sem.at[0])]
+    for i, (start, stop) in enumerate(CHUNKS):
+        part = pl.ds(start, stop - start)
+        loads.append(pltpu.make_async_copy(inverse_ref.at[0, :, part], inv_ref.at[:, part], load_sem.at[i + 1]))
+    small = [pltpu.make_async_copy(source, target, small_sem.at[i]) for i, (source, target) in enumerate(
+        ((labels_hbm, labels_ref), (perm_hbm, perm_ref), (shift_hbm, shift_ref), (probe_hbm, probe_ref)))]
+    for load in loads[:2] + small + loads[2:]:
+        load.start()
     barrier = pltpu.get_barrier_semaphore()
     for device in onward + back:
         pl.semaphore_signal(barrier, inc=1, device_id=device, device_id_type=MESH)
 
     volume = 1.0 / NCELL
     partition, inside = cell_weights()
+    for load in small:
+        load.wait()
     kappa, face = permeability(labels_ref, perm_ref, inside)
     half = [f * (0.5 * volume) for f in face]
     weights = [jnp.concatenate([h * (p + ahead(p, s)) for h, s in zip(half, STRIDES)], axis=1).astype(bf)
                for p in partition]
     probe_rows = split3(probe_ref[...])
 
-    total = None
-    for i in range(CHUNKS):
-        part = pl.ds(i * rows, rows)
-        for load in loads[i]:
-            load.wait()
-        term = jnp.dot(src_ref[:, part], inv_ref[part, :], preferred_element_type=f32)
-        total = term if total is None else total + term
-    snap_ref[...] = total.astype(bf)
+    loads[0].wait()
+    for i, (start, stop) in enumerate(CHUNKS):
+        loads[i + 1].wait()
+        snap_ref[:, start:stop] = jnp.dot(
+            src_ref[...], inv_ref[:, start:stop], preferred_element_type=f32).astype(bf)
     for r in range(0, SNAP, 64):
         field = snap_ref[r:r + 64, :].astype(f32)
         for d, stride in enumerate(STRIDES):
@@ -204,6 +217,29 @@
         first, below, second = g[:128, :128], g[128:, :128], g[128:, 128:]
         diagonal = jnp.sum(jnp.where(row == col, second, 0.0), axis=0, keepdims=True)
         return [jnp.where(row >= col, first, second), below, diagonal]
+
+    def remote(sources, targets, slot, send, recv, device):
+        return pltpu.make_async_remote_copy(
+            src_ref=sources, dst_ref=targets.at[slot], send_sem=send.at[slot], recv_sem=recv.at[slot],
+            device_id=device, device_id_type=MESH)
+
+    def pack(slot, square, below, diagonal):
+        out_ref[slot, 0:128, :] = square.astype(bf)
+        out_ref[slot, 128:256, :] = below.astype(bf)
+        out_ref[slot, 256:272, :] = jnp.broadcast_to(diagonal, (16, 128)).astype(bf)
+
+    def plus(slot, square, below, diagonal):
+        return (square + in_ref[slot, 0:128, :].astype(f32), below + in_ref[slot, 128:256, :].astype(f32),
+                diagonal + in_ref[slot, 256:272, :].astype(f32)[0:1])
+
+    across = {slot: remote(out_ref.at[slot], in_ref, slot, send_sem, recv_sem, device)
+              for slot, device in ((2, onward[0]), (0, onward[0]), (1, onward[1]))}
+    pack(2, *gram(3))
+    pl.semaphore_wait(barrier, 6)
+    across[2].start()
+    upper = gram(2)
+    pack(0, *gram(1))
+    across[0].start()
 
     probed = jnp.dot(probe_rows, snap_ref[...], preferred_element_type=f32)
     probed = probed[0:8] + probed[8:16] + probed[16:24]
@@ -211,34 +247,26 @@
     loaded = jnp.concatenate([probed * (heavy * p) for p in partition], axis=0)
     side = lax.dot_general(split3(loaded), snap_ref[...], NT, preferred_element_type=f32)
     side = side[0:32] + side[32:64] + side[64:96]
-    side = [side[8 * c:8 * c + 8] for c in range(4)]
-
-    copies = {}
-    for slot, corner in ((2, 3), (1, 2), (0, 1)):
-        square, below, diagonal = gram(corner)
-        hi = side[corner].astype(bf).astype(f32)
-        low = side[corner] - hi
-        out_ref[slot, 0:128, :] = square.astype(bf)
-        out_ref[slot, 128:256, :] = below.astype(bf)
-        out_ref[slot, 256:288, :] = jnp.concatenate(
-            [hi[:, :128], hi[:, 128:], low[:, :128], low[:, 128:]], axis=0).astype(bf)
-        out_ref[slot, 288:304, :] = jnp.broadcast_to(diagonal, (16, 128)).astype(bf)
-        copies[slot] = pltpu.make_async_remote_copy(
-            src_ref=out_ref.at[slot], dst_ref=in_ref.at[slot], send_sem=send_sem.at[slot],
-            recv_sem=recv_sem.at[slot], device_id=onward[slot], device_id_type=MESH)
-        if slot == 2:
-            pl.semaphore_wait(barrier, 6)
-        copies[slot].start()
-
-    square, below, diagonal = gram(0)
-    own_side = side[0]
-    for slot in (0, 1, 2):
-        copies[slot].wait_recv()
-        square = square + in_ref[slot, 0:128, :].astype(f32)
-        below = below + in_ref[slot, 128:256, :].astype(f32)
-        t = in_ref[slot, 256:288, :].astype(f32)
-        own_side = own_side + jnp.concatenate([t[0:8] + t[16:24], t[8:16] + t[24:32]], axis=1)
-        diagonal = diagonal + in_ref[slot, 288:304, :].astype(f32)[0:1]
+    side_out_ref[...] = side
+    sides = []
+    for slot in (2, 1, 0):
+        corner = slot + 1
+        sides.append(remote(side_out_ref.at[pl.ds(8 * corner, 8)], side_in_ref, slot, side_send_sem, side_recv_sem,
+                            onward[slot]))
+        sides[-1].start()
+
+    across[2].wait_recv()
+    pack(1, *plus(2, *upper))
+    across[1].start()
+    own = gram(0)
+    own_side = side[0:8]
+    for copy in sides:
+        copy.wait_recv()
+    own_side = own_side + (side_in_ref[0] + side_in_ref[1] + side_in_ref[2])
+    across[0].wait_recv()
+    own = plus(0, *own)
+    across[1].wait_recv()
+    square, below, diagonal = plus(1, *own)
     turned = square.T
     shift = shift_ref[...]
     m_ref[:128, :128] = jnp.where(row >= col, square, turned) + jnp.where(row == col, shift[:, :128], 0.0)
@@ -249,7 +277,7 @@
     m_ref[:, N:] = jnp.concatenate([own_side, jnp.zeros((120, SNAP), f32)], axis=0).T
     eliminate(m_ref)
 
-    solved = m_ref[:, N:].T[0:8]
+    solved = m_ref[:, 128:256].T[0:8]
     coef_ref[0] = solved
     own = solved.astype(bf).astype(f32)
     coef_out_ref[...] = own
@@ -265,13 +293,13 @@
     field = jnp.dot(corners, snap_ref[...], preferred_element_type=f32)
     field = jnp.concatenate([field[8 * c:8 * c + 8] * partition[c] for c in range(4)], axis=0)
     slopes = [ahead(field, stride) - field for stride in STRIDES]
-    left = jnp.concatenate([s * f for s, f in zip(slopes, face)], axis=1)
-    right = jnp.concatenate(slopes, axis=1)
-    element_ref[0] = lax.dot_general(left, right, NT, precision=HI, preferred_element_type=f32)
-    for slot in copies:
-        copies[slot].wait_send()
-    for send in sends:
-        send.wait_send()
+    left = jnp.concatenate(halves(jnp.concatenate([s * f for s, f in zip(slopes, face)], axis=1)), axis=0)
+    right = jnp.concatenate(halves(jnp.concatenate(slopes, axis=1)), axis=0)
+    product = lax.dot_general(left, right, NT, preferred_element_type=f32)
+    product = product[0:32] + product[32:64]
+    element_ref[0] = product[:, 0:32] + product[:, 32:64]
+    for copy in list(across.values()) + sides + sends:
+        copy.wait_send()
 
 
 def scale_kernel(coef_ref, element_ref, coef_out_ref, element_out_ref):
@@ -284,20 +312,28 @@
     coef, element = pl.pallas_call(
         functools.partial(basis_kernel, size),
         out_shape=shapes,
-        in_specs=[VMEM, pl.BlockSpec(memory_space=pltpu.SMEM), pl.BlockSpec(memory_space=pl.ANY),
-                  pl.BlockSpec(memory_space=pl.ANY), VMEM, VMEM],
+        in_specs=[pl.BlockSpec(memory_space=pl.ANY)] * 6,
         out_specs=(VMEM, VMEM),
         scratch_shapes=[
+            pltpu.VMEM((1, NCELL), jnp.int32),
+            pltpu.VMEM((1, PHASES), f32),
+            pltpu.VMEM((1, SNAP), f32),
+            pltpu.VMEM((NBASIS, SNAP), f32),
             pltpu.VMEM((NCELL, NCELL), bf),
             pltpu.VMEM((SNAP, NCELL), bf),
             pltpu.VMEM((SNAP, NCELL), bf),
             pltpu.VMEM((SNAP, 3 * NCELL), bf),
             pltpu.VMEM((3, PACK, 128), bf),
             pltpu.VMEM((3, PACK, 128), bf),
+            pltpu.VMEM((4 * NBASIS, SNAP), f32),
+            pltpu.VMEM((3, NBASIS, SNAP), f32),
             pltpu.VMEM((N, W), f32),
             pltpu.VMEM((NBASIS, SNAP), f32),
             pltpu.VMEM((3, NBASIS, SNAP), f32),
-            pltpu.SemaphoreType.DMA((2, CHUNKS)),
+            pltpu.SemaphoreType.DMA((4,)),
+            pltpu.SemaphoreType.DMA((1 + len(CHUNKS),)),
+            pltpu.SemaphoreType.DMA((3,)),
+            pltpu.SemaphoreType.DMA((3,)),
             pltpu.SemaphoreType.DMA((3,)),
             pltpu.SemaphoreType.DMA((3,)),
             pltpu.SemaphoreType.DMA((3,)),
@@ -305,7 +341,7 @@
         ],
         compiler_params=pltpu.CompilerParams(collective_id=0, has_side_effects=True),
         name="basis",
-    )(phase_labels, phase_perm, local_inverse, sources, shift, probe.T)
+    )(phase_labels, phase_perm.reshape(1, PHASES), local_inverse, sources, shift, probe.T)
     coef, element = pl.pallas_call(
         scale_kernel, out_shape=shapes, in_specs=[VMEM, VMEM], out_specs=(VMEM, VMEM), name="scale",
     )(coef, element)

time: 35.8 us -> 38.2 us (1.067)
  the two profiles are of different devices: /device:TPU:31 before, /device:TPU:23 now
where the time goes in v4:
time: 38.2 us; the launch traced here: 38 us
  Pallas kernels  37.4 us (98%)
  between operations  0.64 us (2%)
    pallas_call x1, Pallas kernels, local(): pl.pallas_call(functools.partial(basis_kernel, size), out_shape=shapes, i...  36 us
    pallas_call x1, Pallas kernels, local(): pl.pallas_call(scale_kernel, out_shape=shapes, in_specs=[VMEM, VMEM], out...  1.35 us

profile of v4, /device:TPU:23, one launch (start us, length us, event | category | flops | bytes accessed | tf_op | source)
XLA Modules:
  0.0 38.0 jit_solution(4787454283700380816)
XLA Ops:
  0.6 36.0 %basis.1 = (f32[1,8,256]{2,1,0:T(8,128)}, f32[1,32,32]{2,1,0:T(8,128)}) custom-call(s32[1,1152]{1,0:T(1,128)} %labels_hbm.1, f32[1,3]{1,0:T(1,128)} %bitcast.4, bf16[1,1152,1152]{2,1,0:T(8,128)(2,1)} %inverse_ref.1, bf16[1,256,1152]{2,1,0:T(8,128)(2,1)} %sources_ref.1, f32[1,256]{1,0:T(1,128)} %shift_hbm.1, f32[8,256]{1,0:T(8,128)} %bitcast.3), custom_call_target="tpu_custom_call" | custom-call | tf_op jit(solution)/shard_map/basis/pallas_call | solution.py:312
  36.7 1.3 %scale.1 = (f32[1,8,256]{2,1,0:T(8,128)}, f32[1,32,32]{2,1,0:T(8,128)}) custom-call(f32[1,8,256]{2,1,0:T(8,128)} %get-tuple-element.6.coef_ref, f32[1,32,32]{2,1,0:T(8,128)} %get-tuple-element.7.element_ref), custom_call_target="tpu_custom_call" | custom-call | tf_op jit(solution)/shard_map/scale/pallas_call | solution.py:345

commit v5 on v4

--- a/solution.py
+++ b/solution.py
@@ -186,7 +186,7 @@
     for load in loads[:2] + small + loads[2:]:
         load.start()
     barrier = pltpu.get_barrier_semaphore()
-    for device in onward + back:
+    for device in back:
         pl.semaphore_signal(barrier, inc=1, device_id=device, device_id_type=MESH)
 
     volume = 1.0 / NCELL
@@ -205,9 +205,9 @@
         snap_ref[:, start:stop] = jnp.dot(
             src_ref[...], inv_ref[:, start:stop], preferred_element_type=f32).astype(bf)
     for r in range(0, SNAP, 64):
-        field = snap_ref[r:r + 64, :].astype(f32)
+        field = snap_ref[r:r + 64, :]
         for d, stride in enumerate(STRIDES):
-            grad_ref[r:r + 64, d * NCELL:(d + 1) * NCELL] = (ahead(field, stride) - field).astype(bf)
+            grad_ref[r:r + 64, d * NCELL:(d + 1) * NCELL] = ahead(field, stride) - field
 
     row = lax.broadcasted_iota(jnp.int32, (128, 128), 0)
     col = lax.broadcasted_iota(jnp.int32, (128, 128), 1)
@@ -232,14 +232,13 @@
         return (square + in_ref[slot, 0:128, :].astype(f32), below + in_ref[slot, 128:256, :].astype(f32),
                 diagonal + in_ref[slot, 256:272, :].astype(f32)[0:1])
 
-    across = {slot: remote(out_ref.at[slot], in_ref, slot, send_sem, recv_sem, device)
-              for slot, device in ((2, onward[0]), (0, onward[0]), (1, onward[1]))}
-    pack(2, *gram(3))
-    pl.semaphore_wait(barrier, 6)
+    across = [remote(out_ref.at[slot], in_ref, slot, send_sem, recv_sem, onward[slot]) for slot in range(3)]
+    both = gram(3), gram(2)
+    pack(2, *both[0])
+    pack(1, *both[1])
+    pl.semaphore_wait(barrier, 3)
     across[2].start()
-    upper = gram(2)
-    pack(0, *gram(1))
-    across[0].start()
+    across[1].start()
 
     probed = jnp.dot(probe_rows, snap_ref[...], preferred_element_type=f32)
     probed = probed[0:8] + probed[8:16] + probed[16:24]
@@ -255,18 +254,17 @@
                             onward[slot]))
         sides[-1].start()
 
-    across[2].wait_recv()
-    pack(1, *plus(2, *upper))
-    across[1].start()
-    own = gram(0)
+    beside, own = gram(1), gram(0)
+    pack(0, *beside)
+    across[0].start()
     own_side = side[0:8]
     for copy in sides:
         copy.wait_recv()
     own_side = own_side + (side_in_ref[0] + side_in_ref[1] + side_in_ref[2])
-    across[0].wait_recv()
-    own = plus(0, *own)
-    across[1].wait_recv()
-    square, below, diagonal = plus(1, *own)
+    for slot in (0, 2, 1):
+        across[slot].wait_recv()
+        own = plus(slot, *own)
+    square, below, diagonal = own
     turned = square.T
     shift = shift_ref[...]
     m_ref[:128, :128] = jnp.where(row >= col, square, turned) + jnp.where(row == col, shift[:, :128], 0.0)
@@ -295,10 +293,11 @@
     slopes = [ahead(field, stride) - field for stride in STRIDES]
     left = jnp.concatenate(halves(jnp.concatenate([s * f for s, f in zip(slopes, face)], axis=1)), axis=0)
     right = jnp.concatenate(halves(jnp.concatenate(slopes, axis=1)), axis=0)
-    product = lax.dot_general(left, right, NT, preferred_element_type=f32)
+    product = (lax.dot_general(left[:, :1792], right[:, :1792], NT, preferred_element_type=f32)
+               + lax.dot_general(left[:, 1792:], right[:, 1792:], NT, preferred_element_type=f32))
     product = product[0:32] + product[32:64]
     element_ref[0] = product[:, 0:32] + product[:, 32:64]
-    for copy in list(across.values()) + sides + sends:
+    for copy in across + sides + sends:
         copy.wait_send()
 
 

time: 38.2 us -> 37 us (0.969)
  the two profiles are of different devices: /device:TPU:23 before, /device:TPU:63 now
where the time goes in v5:
time: 37 us; the launch traced here: 36.8 us
  Pallas kernels  36.2 us (98%)
  between operations  0.64 us (2%)
    pallas_call x1, Pallas kernels, local(): pl.pallas_call(functools.partial(basis_kernel, size), out_shape=shapes, i...  34.9 us
    pallas_call x1, Pallas kernels, local(): pl.pallas_call(scale_kernel, out_shape=shapes, in_specs=[VMEM, VMEM], out...  1.35 us

profile of v5, /device:TPU:63, one launch (start us, length us, event | category | flops | bytes accessed | tf_op | source)
XLA Modules:
  0.0 36.8 jit_solution(5667744235087431860)
XLA Ops:
  0.6 34.9 %basis.1 = (f32[1,8,256]{2,1,0:T(8,128)}, f32[1,32,32]{2,1,0:T(8,128)}) custom-call(s32[1,1152]{1,0:T(1,128)} %labels_hbm.1, f32[1,3]{1,0:T(1,128)} %bitcast.4, bf16[1,1152,1152]{2,1,0:T(8,128)(2,1)} %inverse_ref.1, bf16[1,256,1152]{2,1,0:T(8,128)(2,1)} %sources_ref.1, f32[1,256]{1,0:T(1,128)} %shift_hbm.1, f32[8,256]{1,0:T(8,128)} %bitcast.3), custom_call_target="tpu_custom_call" | custom-call | tf_op jit(solution)/shard_map/basis/pallas_call | solution.py:311
  35.5 1.3 %scale.1 = (f32[1,8,256]{2,1,0:T(8,128)}, f32[1,32,32]{2,1,0:T(8,128)}) custom-call(f32[1,8,256]{2,1,0:T(8,128)} %get-tuple-element.6.coef_ref, f32[1,32,32]{2,1,0:T(8,128)} %get-tuple-element.7.element_ref), custom_call_target="tpu_custom_call" | custom-call | tf_op jit(solution)/shard_map/scale/pallas_call | solution.py:344

commit v6 on v5

--- a/solution.py
+++ b/solution.py
@@ -174,7 +174,7 @@
 
 def basis_kernel(size, labels_hbm, perm_hbm, inverse_ref, sources_ref, shift_hbm, probe_hbm,
                  coef_ref, element_ref, labels_ref, perm_ref, shift_ref, probe_ref, inv_ref, src_ref, snap_ref,
-                 grad_ref, out_ref, in_ref, side_out_ref, side_in_ref, m_ref, coef_out_ref, coef_in_ref,
+                 grad_ref, out_ref, in_ref, side_out_ref, side_in_ref, sum_ref, m_ref, coef_out_ref, coef_in_ref,
                  small_sem, load_sem, send_sem, recv_sem, side_send_sem, side_recv_sem, coef_send_sem, coef_recv_sem):
     onward, back = neighbours(size, 1), neighbours(size, -1)
     loads = [pltpu.make_async_copy(sources_ref.at[0], src_ref, load_sem.at[0])]
@@ -232,13 +232,21 @@
         return (square + in_ref[slot, 0:128, :].astype(f32), below + in_ref[slot, 128:256, :].astype(f32),
                 diagonal + in_ref[slot, 256:272, :].astype(f32)[0:1])
 
-    across = [remote(out_ref.at[slot], in_ref, slot, send_sem, recv_sem, onward[slot]) for slot in range(3)]
+    grps, subs = size
+    g, s = lax.axis_index("grp"), lax.axis_index("sub")
+    parity = lax.rem(s, 2)
+    far = (lax.rem(g + parity, grps), lax.rem(s + 1, subs))
+    across = [remote(out_ref.at[slot], in_ref, slot, send_sem, recv_sem, device)
+              for slot, device in enumerate((onward[0], onward[1], far))]
     both = gram(3), gram(2)
     pack(2, *both[0])
-    pack(1, *both[1])
     pl.semaphore_wait(barrier, 3)
     across[2].start()
-    across[1].start()
+
+    @pl.when(parity == 0)
+    def _():
+        pack(1, *both[1])
+        across[1].start()
 
     probed = jnp.dot(probe_rows, snap_ref[...], preferred_element_type=f32)
     probed = probed[0:8] + probed[8:16] + probed[16:24]
@@ -254,17 +262,34 @@
                             onward[slot]))
         sides[-1].start()
 
+    @pl.when(parity == 1)
+    def _():
+        across[2].wait_recv()
+        pack(1, *plus(2, *both[1]))
+        across[1].start()
+
     beside, own = gram(1), gram(0)
     pack(0, *beside)
+    across[2].wait_send()
+    across[1].wait_send()
     across[0].start()
     own_side = side[0:8]
     for copy in sides:
         copy.wait_recv()
     own_side = own_side + (side_in_ref[0] + side_in_ref[1] + side_in_ref[2])
-    for slot in (0, 2, 1):
+    for slot in (0, 1):
         across[slot].wait_recv()
         own = plus(slot, *own)
-    square, below, diagonal = own
+    sum_ref[0:128, :] = own[0]
+    sum_ref[128:256, :] = own[1]
+    sum_ref[256:264, :] = jnp.broadcast_to(own[2], (8, 128))
+
+    @pl.when(parity == 0)
+    def _():
+        across[2].wait_recv()
+        sum_ref[...] = sum_ref[...] + in_ref[2, 0:264, :].astype(f32)
+
+    square, below, diagonal = sum_ref[0:128, :], sum_ref[128:256, :], sum_ref[256:257, :]
     turned = square.T
     shift = shift_ref[...]
     m_ref[:128, :128] = jnp.where(row >= col, square, turned) + jnp.where(row == col, shift[:, :128], 0.0)
@@ -297,7 +322,7 @@
                + lax.dot_general(left[:, 1792:], right[:, 1792:], NT, preferred_element_type=f32))
     product = product[0:32] + product[32:64]
     element_ref[0] = product[:, 0:32] + product[:, 32:64]
-    for copy in across + sides + sends:
+    for copy in across[:1] + sides + sends:
         copy.wait_send()
 
 
@@ -326,6 +351,7 @@
             pltpu.VMEM((3, PACK, 128), bf),
             pltpu.VMEM((4 * NBASIS, SNAP), f32),
             pltpu.VMEM((3, NBASIS, SNAP), f32),
+            pltpu.VMEM((264, 128), f32),
             pltpu.VMEM((N, W), f32),
             pltpu.VMEM((NBASIS, SNAP), f32),
             pltpu.VMEM((3, NBASIS, SNAP), f32),

time: 37 us -> 34.4 us (0.930)
  the two profiles are of different devices: /device:TPU:63 before, /device:TPU:31 now
where the time goes in v6:
time: 34.4 us; the launch traced here: 34.2 us
  Pallas kernels  33.6 us (98%)
  between operations  0.64 us (2%)
    pallas_call x1, Pallas kernels, local(): pl.pallas_call(functools.partial(basis_kernel, size), out_shape=shapes, i...  32.2 us
    pallas_call x1, Pallas kernels, local(): pl.pallas_call(scale_kernel, out_shape=shapes, in_specs=[VMEM, VMEM], out...  1.35 us

profile of v6, /device:TPU:31, one launch (start us, length us, event | category | flops | bytes accessed | tf_op | source)
XLA Modules:
  0.0 34.2 jit_solution(15686339723674283809)
XLA Ops:
  0.6 32.2 %basis.1 = (f32[1,8,256]{2,1,0:T(8,128)}, f32[1,32,32]{2,1,0:T(8,128)}) custom-call(s32[1,1152]{1,0:T(1,128)} %labels_hbm.1, f32[1,3]{1,0:T(1,128)} %bitcast.4, bf16[1,1152,1152]{2,1,0:T(8,128)(2,1)} %inverse_ref.1, bf16[1,256,1152]{2,1,0:T(8,128)(2,1)} %sources_ref.1, f32[1,256]{1,0:T(1,128)} %shift_hbm.1, f32[8,256]{1,0:T(8,128)} %bitcast.3), custom_call_target="tpu_custom_call" | custom-call | tf_op jit(solution)/shard_map/basis/pallas_call | solution.py:336
  32.8 1.3 %scale.1 = (f32[1,8,256]{2,1,0:T(8,128)}, f32[1,32,32]{2,1,0:T(8,128)}) custom-call(f32[1,8,256]{2,1,0:T(8,128)} %get-tuple-element.6.coef_ref, f32[1,32,32]{2,1,0:T(8,128)} %get-tuple-element.7.element_ref), custom_call_target="tpu_custom_call" | custom-call | tf_op jit(solution)/shard_map/scale/pallas_call | solution.py:370

commit v7 on v6

--- a/solution.py
+++ b/solution.py
@@ -190,23 +190,26 @@
         pl.semaphore_signal(barrier, inc=1, device_id=device, device_id_type=MESH)
 
     volume = 1.0 / NCELL
+
+    def snapshots(start, stop):
+        snap_ref[:, start:stop] = jnp.dot(
+            src_ref[...], inv_ref[:, start:stop], preferred_element_type=f32).astype(bf)
+
+    for load in loads[:2] + small:
+        load.wait()
+    snapshots(*CHUNKS[0])
     partition, inside = cell_weights()
-    for load in small:
-        load.wait()
     kappa, face = permeability(labels_ref, perm_ref, inside)
     half = [f * (0.5 * volume) for f in face]
     weights = [jnp.concatenate([h * (p + ahead(p, s)) for h, s in zip(half, STRIDES)], axis=1).astype(bf)
                for p in partition]
     probe_rows = split3(probe_ref[...])
-
-    loads[0].wait()
-    for i, (start, stop) in enumerate(CHUNKS):
-        loads[i + 1].wait()
-        snap_ref[:, start:stop] = jnp.dot(
-            src_ref[...], inv_ref[:, start:stop], preferred_element_type=f32).astype(bf)
-    for r in range(0, SNAP, 64):
-        field = snap_ref[r:r + 64, :]
-        for d, stride in enumerate(STRIDES):
+    for load, chunk in zip(loads[2:], CHUNKS[1:]):
+        load.wait()
+        snapshots(*chunk)
+    for d, stride in enumerate(STRIDES):
+        for r in range(0, SNAP, 64):
+            field = snap_ref[r:r + 64, :]
             grad_ref[r:r + 64, d * NCELL:(d + 1) * NCELL] = ahead(field, stride) - field
 
     row = lax.broadcasted_iota(jnp.int32, (128, 128), 0)
@@ -321,21 +324,16 @@
     product = (lax.dot_general(left[:, :1792], right[:, :1792], NT, preferred_element_type=f32)
                + lax.dot_general(left[:, 1792:], right[:, 1792:], NT, preferred_element_type=f32))
     product = product[0:32] + product[32:64]
-    element_ref[0] = product[:, 0:32] + product[:, 32:64]
+    element_ref[0] = (product[:, 0:32] + product[:, 32:64]) * (1.0 / (NCELL * SNAP))
     for copy in across[:1] + sides + sends:
         copy.wait_send()
-
-
-def scale_kernel(coef_ref, element_ref, coef_out_ref, element_out_ref):
-    coef_out_ref[...] = coef_ref[...]
-    element_out_ref[...] = element_ref[...] * (1.0 / (NCELL * SNAP))
 
 
 def local(size, phase_labels, phase_perm, local_inverse, sources, shift, probe):
     shapes = (jax.ShapeDtypeStruct((1, NBASIS, SNAP), f32), jax.ShapeDtypeStruct((1, 32, 32), f32))
     coef, element = pl.pallas_call(
         functools.partial(basis_kernel, size),
-        out_shape=shapes,
+        out_shape=tuple(pltpu.VMEM(shape.shape, shape.dtype) for shape in shapes),
         in_specs=[pl.BlockSpec(memory_space=pl.ANY)] * 6,
         out_specs=(VMEM, VMEM),
         scratch_shapes=[
@@ -367,9 +365,6 @@
         compiler_params=pltpu.CompilerParams(collective_id=0, has_side_effects=True),
         name="basis",
     )(phase_labels, phase_perm.reshape(1, PHASES), local_inverse, sources, shift, probe.T)
-    coef, element = pl.pallas_call(
-        scale_kernel, out_shape=shapes, in_specs=[VMEM, VMEM], out_specs=(VMEM, VMEM), name="scale",
-    )(coef, element)
     return (coef.transpose(0, 2, 1), element)
 
 

time: 34.4 us -> 33.3 us (0.968)
  Pallas kernels: 33.6 us -> 31.3 us
  local copies, waits for them, and re-layouts: 0 us -> 1.21 us
    pallas_call x2 -> x1, Pallas kernels: 33.6 us -> 31.3 us  [local(): pl.pallas_call(functools.partial(basis_kernel, size), out_shape=tuple((pl...]
    unnamed x0 -> x2, local copies, waits for them, and re-layouts: none -> 1.21 us
where the time goes in v7:
time: 33.3 us; the launch traced here: 33.2 us
  Pallas kernels  31.3 us (94%)
  local copies, waits for them, and re-layouts  1.21 us (4%)
  between operations  0.64 us (2%)
    pallas_call x1, Pallas kernels, local(): pl.pallas_call(functools.partial(basis_kernel, size), out_shape=tuple((pl...  31.3 us
    unnamed x2, local copies, waits for them, and re-layouts  1.21 us

profile of v7, /device:TPU:31, one launch (start us, length us, event | category | flops | bytes accessed | tf_op | source)
XLA Modules:
  0.0 33.2 jit_solution(5523702671839689077)
XLA Ops:
  0.6 31.3 %basis.1 = (f32[1,8,256]{2,1,0:T(8,128)S(1)}, f32[1,32,32]{2,1,0:T(8,128)S(1)}) custom-call(s32[1,1152]{1,0:T(1,128)} %labels_hbm.1, f32[1,3]{1,0:T(1,128)} %bitcast.5, bf16[1,1152,1152]{2,1,0:T(8,128)(2,1)} %inverse_ref.1, bf16[1,256,1152]{2,1,0:T(8,128)(2,1)} %sources_ref.1, f32[1,256]{1,0:T(1,128)} %shift_hbm.1, f32[8,256]{1,0:T(8,128)} %bitcast.4), custom_call_target="tpu_custom_call" | custom-call | tf_op jit(solution)/shard_map/basis/pallas_call | solution.py:334
  32.0 0.6 %copy.10 = f32[1,256,8]{1,2,0:T(8,128)} copy(f32[1,256,8]{1,2,0:T(8,128)S(1)} %bitcast.3) | data formatting | bytes 16384
  32.6 0.6 %copy.11 = f32[1,32,32]{2,1,0:T(8,128)} copy(f32[1,32,32]{2,1,0:T(8,128)S(1)} %get-tuple-element.7) | data formatting | bytes 8192

commit v8 on v7

--- a/solution.py
+++ b/solution.py
@@ -329,6 +329,15 @@
         copy.wait_send()
 
 
+def hand_out_kernel(coef_ref, element_ref, coef_out_ref, element_out_ref, sem):
+    copies = [pltpu.make_async_copy(coef_ref, coef_out_ref, sem.at[0]),
+              pltpu.make_async_copy(element_ref, element_out_ref, sem.at[1])]
+    for copy in copies:
+        copy.start()
+    for copy in copies:
+        copy.wait()
+
+
 def local(size, phase_labels, phase_perm, local_inverse, sources, shift, probe):
     shapes = (jax.ShapeDtypeStruct((1, NBASIS, SNAP), f32), jax.ShapeDtypeStruct((1, 32, 32), f32))
     coef, element = pl.pallas_call(
@@ -365,6 +374,14 @@
         compiler_params=pltpu.CompilerParams(collective_id=0, has_side_effects=True),
         name="basis",
     )(phase_labels, phase_perm.reshape(1, PHASES), local_inverse, sources, shift, probe.T)
+    coef, element = pl.pallas_call(
+        hand_out_kernel,
+        out_shape=shapes,
+        in_specs=[VMEM, VMEM],
+        out_specs=(pl.BlockSpec(memory_space=pl.ANY), pl.BlockSpec(memory_space=pl.ANY)),
+        scratch_shapes=[pltpu.SemaphoreType.DMA((2,))],
+        name="hand_out",
+    )(*(pltpu.with_memory_space_constraint(x, pltpu.VMEM) for x in (coef, element)))
     return (coef.transpose(0, 2, 1), element)
 
 

time: 33.3 us -> 32.7 us (0.982)
  local copies, waits for them, and re-layouts: 1.21 us -> 0 us
  Pallas kernels: 31.3 us -> 32 us
    unnamed x2 -> x0, local copies, waits for them, and re-layouts: 1.21 us -> none
    pallas_call x0 -> x1, Pallas kernels: none -> 0.63 us  [local(): pl.pallas_call(hand_out_kernel, out_shape=shapes, in_specs=[VMEM, VMEM],...]
where the time goes in v8:
time: 32.7 us; the launch traced here: 32.6 us
  Pallas kernels  32 us (98%)
  between operations  0.64 us (2%)
    pallas_call x1, Pallas kernels, local(): pl.pallas_call(functools.partial(basis_kernel, size), out_shape=tuple((pl...  31.3 us

profile of v8, /device:TPU:31, one launch (start us, length us, event | category | flops | bytes accessed | tf_op | source)
XLA Modules:
  0.0 32.6 jit_solution(9751813914617184563)
XLA Ops:
  0.6 31.3 %basis.1 = (f32[1,8,256]{2,1,0:T(8,128)S(1)}, f32[1,32,32]{2,1,0:T(8,128)S(1)}) custom-call(s32[1,1152]{1,0:T(1,128)} %labels_hbm.1, f32[1,3]{1,0:T(1,128)} %bitcast.4, bf16[1,1152,1152]{2,1,0:T(8,128)(2,1)} %inverse_ref.1, bf16[1,256,1152]{2,1,0:T(8,128)(2,1)} %sources_ref.1, f32[1,256]{1,0:T(1,128)} %shift_hbm.1, f32[8,256]{1,0:T(8,128)} %bitcast.3), custom_call_target="tpu_custom_call" | custom-call | tf_op jit(solution)/shard_map/basis/pallas_call | solution.py:343
  32.0 0.6 %hand_out.1 = (f32[1,8,256]{2,1,0:T(8,128)}, f32[1,32,32]{2,1,0:T(8,128)}) custom-call(f32[1,8,256]{2,1,0:T(8,128)S(1)} %get-tuple-element.6.coef_ref, f32[1,32,32]{2,1,0:T(8,128)S(1)} %get-tuple-element.7.element_ref), custom_call_target="tpu_custom_call" | custom-call | tf_op jit(solution)/shard_map/hand_out/pallas_call | solution.py:377

commit v9 on v8

--- a/solution.py
+++ b/solution.py
@@ -100,14 +100,14 @@
         width = 128 * len(live)
         gap = lambda n: [jnp.zeros((n, width), bf)] if n else []
         right = jnp.concatenate(
-            [piece for x in (hi, hi, low, low) for piece in gap(off) + [x] + gap(128 - off - NB)], axis=0)
+            [piece for x in (hi, hi, low) for piece in gap(off) + [x] + gap(128 - off - NB)], axis=0)
         lo = live[0] * 128
 
         def update(r0, r1):
             if r1 <= r0:
                 return
             lhi, llow = halves(m_ref[r0:r1, 128 * t0:128 * t0 + 128])
-            left = jnp.concatenate([lhi, llow, lhi, llow], axis=1)
+            left = jnp.concatenate([lhi, llow, lhi], axis=1)
             got = m_ref[r0:r1, lo:lo + width] - jnp.dot(left, right, preferred_element_type=f32)
             pieces = moved(k, {t: got[:, 128 * i:128 * i + 128] for i, t in enumerate(live)})
             for t in pieces:
@@ -197,7 +197,9 @@
 
     for load in loads[:2] + small:
         load.wait()
-    snapshots(*CHUNKS[0])
+    for r in (0, 128):
+        snap_ref[r:r + 128, 0:CHUNKS[0][1]] = jnp.dot(
+            src_ref[r:r + 128, :], inv_ref[:, 0:CHUNKS[0][1]], preferred_element_type=f32).astype(bf)
     partition, inside = cell_weights()
     kappa, face = permeability(labels_ref, perm_ref, inside)
     half = [f * (0.5 * volume) for f in face]

time: 32.7 us -> 32.6 us (level)
  no operation moved by 1% of the time
where the time goes in v9:
time: 32.6 us; the launch traced here: 32.5 us
  Pallas kernels  31.8 us (98%)
  between operations  0.64 us (2%)
    pallas_call x1, Pallas kernels, local(): pl.pallas_call(functools.partial(basis_kernel, size), out_shape=tuple((pl...  31.2 us

profile of v9, /device:TPU:31, one launch (start us, length us, event | category | flops | bytes accessed | tf_op | source)
XLA Modules:
  0.0 32.5 jit_solution(10949862069270019917)
XLA Ops:
  0.6 31.2 %basis.1 = (f32[1,8,256]{2,1,0:T(8,128)S(1)}, f32[1,32,32]{2,1,0:T(8,128)S(1)}) custom-call(s32[1,1152]{1,0:T(1,128)} %labels_hbm.1, f32[1,3]{1,0:T(1,128)} %bitcast.4, bf16[1,1152,1152]{2,1,0:T(8,128)(2,1)} %inverse_ref.1, bf16[1,256,1152]{2,1,0:T(8,128)(2,1)} %sources_ref.1, f32[1,256]{1,0:T(1,128)} %shift_hbm.1, f32[8,256]{1,0:T(8,128)} %bitcast.3), custom_call_target="tpu_custom_call" | custom-call | tf_op jit(solution)/shard_map/basis/pallas_call | solution.py:345
  31.8 0.6 %hand_out.1 = (f32[1,8,256]{2,1,0:T(8,128)}, f32[1,32,32]{2,1,0:T(8,128)}) custom-call(f32[1,8,256]{2,1,0:T(8,128)S(1)} %get-tuple-element.6.coef_ref, f32[1,32,32]{2,1,0:T(8,128)S(1)} %get-tuple-element.7.element_ref), custom_call_target="tpu_custom_call" | custom-call | tf_op jit(solution)/shard_map/hand_out/pallas_call | solution.py:379

commit v10 on v9

--- a/solution.py
+++ b/solution.py
@@ -251,7 +251,6 @@
     @pl.when(parity == 0)
     def _():
         pack(1, *both[1])
-        across[1].start()
 
     probed = jnp.dot(probe_rows, snap_ref[...], preferred_element_type=f32)
     probed = probed[0:8] + probed[8:16] + probed[16:24]
@@ -271,8 +270,8 @@
     def _():
         across[2].wait_recv()
         pack(1, *plus(2, *both[1]))
-        across[1].start()
-
+
+    across[1].start()
     beside, own = gram(1), gram(0)
     pack(0, *beside)
     across[2].wait_send()

time: 32.6 us -> 32.3 us (level)
  the two profiles are of different devices: /device:TPU:31 before, /device:TPU:63 now
where the time goes in v10:
time: 32.3 us; the launch traced here: 32.2 us
  Pallas kernels  31.6 us (98%)
  between operations  0.64 us (2%)
    pallas_call x1, Pallas kernels, local(): pl.pallas_call(functools.partial(basis_kernel, size), out_shape=tuple((pl...  31 us

profile of v10, /device:TPU:63, one launch (start us, length us, event | category | flops | bytes accessed | tf_op | source)
XLA Modules:
  0.0 32.2 jit_solution(2725195804980979303)
XLA Ops:
  0.6 31.0 %basis.1 = (f32[1,8,256]{2,1,0:T(8,128)S(1)}, f32[1,32,32]{2,1,0:T(8,128)S(1)}) custom-call(s32[1,1152]{1,0:T(1,128)} %labels_hbm.1, f32[1,3]{1,0:T(1,128)} %bitcast.4, bf16[1,1152,1152]{2,1,0:T(8,128)(2,1)} %inverse_ref.1, bf16[1,256,1152]{2,1,0:T(8,128)(2,1)} %sources_ref.1, f32[1,256]{1,0:T(1,128)} %shift_hbm.1, f32[8,256]{1,0:T(8,128)} %bitcast.3), custom_call_target="tpu_custom_call" | custom-call | tf_op jit(solution)/shard_map/basis/pallas_call | solution.py:344
  31.6 0.6 %hand_out.1 = (f32[1,8,256]{2,1,0:T(8,128)}, f32[1,32,32]{2,1,0:T(8,128)}) custom-call(f32[1,8,256]{2,1,0:T(8,128)S(1)} %get-tuple-element.6.coef_ref, f32[1,32,32]{2,1,0:T(8,128)S(1)} %get-tuple-element.7.element_ref), custom_call_target="tpu_custom_call" | custom-call | tf_op jit(solution)/shard_map/hand_out/pallas_call | solution.py:378
